TPU v7x, 256 devices: a whole 4x4x8 slice. The times are simulated.
256 devices in a mesh: drift: 16 (over x_lo, y, core), wire: 16 (over x_hi, z).
Axes of the slice: x: 4 (x_hi: 2, x_lo: 2; x = x_hi * 2 + x_lo), y: 4, z: 8, core: 2. Of those that a mesh axis runs over, the one named last changes fastest.
Arguments:
- features: bfloat16 [16, 16, 576, 128], P('drift', 'wire'), may hold values from -6 to 6
- first_weight: bfloat16 [27, 128, 128], replicated, may hold values from -0.109375 to 0.109375
- second_weight: bfloat16 [27, 128, 128], replicated, may hold values from -0.109375 to 0.109375
- cotangent: bfloat16 [16, 16, 576, 128], P('drift', 'wire'), may hold values from -6 to 6
- counts: int32 [16, 16], P('drift', 'wire'), may hold values from 1 to 9, as said below
- kernel_map: int32 [16, 16, 27, 9], P('drift', 'wire'), may hold values from 0 to 25, as said below
- send_lists: int32 [16, 16, 16], P('drift', 'wire'), may hold values from 0 to 9, as said below
Outputs:
- output: bfloat16 [16, 16, 576, 128], P('drift', 'wire')
- grad_features: bfloat16 [16, 16, 576, 128], P('drift', 'wire')
- grad_first: float32 [27, 128, 128], replicated
- grad_second: float32 [27, 128, 128], replicated
Inputs may be any that keep to these rules, and one draw needn't show every extreme that they name: Slots below counts[i, j] hold the region's active blocks in order of position; some region has all 9 positions active and some region exactly one. kernel_map[i, j, k, s] is the block_table row of the active block at block offset k of slot s: a slot below 9 for a block of the same region, 10 + a segment position for a block of a neighbouring region (listed there in that region's send list), and 9 where that block is inactive, outside the volume, or s is an empty slot. `send_lists`: each segment lists, in order of position, the positions of the region's face, edge or corner next to that neighbour: the slot of an active block there, else 9.
All inputs are finite; a program needn't handle non-finite values.
Results may differ from a plain program's by a relative error of at most 0.0031.
Values may be sent and summed in bfloat16 or wider, within the bound.
A program may use at most 128 MiB of HBM per device.

v0:
```python
import math

import jax
import jax.numpy as jnp
from jax import lax
from jax.sharding import PartitionSpec as P

BX = 3
BW = 3
BZ = 1


DIRECTIONS = ((-1, 0), (1, 0), (0, -1), (0, 1), (-1, -1), (-1, 1), (1, -1), (1, 1))


def from_behind(value, axis, steps):
    count = lax.axis_size(axis)
    initial, last = (max(0, -steps), min(count, count - steps))
    return lax.ppermute(value, axis, [(source, source + steps) for source in range(initial, last)])


def segment_length(drift_step, wire_step):
    return (BX if drift_step == 0 else 1) * (BW if wire_step == 0 else 1) * BZ


def segment_start(drift_step, wire_step):
    first_row = 0
    for direction in DIRECTIONS:
        if direction == (drift_step, wire_step):
            return first_row
        first_row = first_row + segment_length(direction[0], direction[1])
    return first_row


def voxel_span(step_value):
    if step_value < 0:
        return slice(3, 4)
    if step_value == 0:
        return slice(0, 4)
    return slice(0, 1)


def neighbourhood(block_table, kernel_rows):
    planes = []
    for step_x in (-1, 0, 1):
        columns = []
        for step_y in (-1, 0, 1):
            pieces = []
            for step_z in (-1, 0, 1):
                offset = 9 * (step_x + 1) + 3 * (step_y + 1) + (step_z + 1)
                sliced = block_table[
                    :, voxel_span(step_x), voxel_span(step_y), voxel_span(step_z), :
                ]
                pieces.append(jnp.take(sliced, kernel_rows[offset], axis=0))
            columns.append(jnp.concatenate(pieces, axis=3))
        planes.append(jnp.concatenate(columns, axis=2))
    return jnp.concatenate(planes, axis=1)


def gather_columns(window, shift_x):
    block_count = window.shape[0]
    channels = window.shape[-1]
    pieces = []
    for shift_y in range(3):
        for shift_z in range(3):
            sliced = window[
                :, shift_x : shift_x + 4, shift_y : shift_y + 4, shift_z : shift_z + 4, :
            ]
            pieces.append(sliced.reshape(block_count * 64, channels))
    return jnp.concatenate(pieces, axis=1)


def convolve(window, weight):
    channels = window.shape[-1]
    summed = jnp.zeros((window.shape[0] * 64, weight.shape[2]), jnp.float32)
    for shift_x in range(3):
        stacked = gather_columns(window, shift_x)
        matrix = weight[9 * shift_x : 9 * shift_x + 9].reshape(9 * channels, weight.shape[2])
        summed = summed + jnp.dot(stacked, matrix, preferred_element_type=jnp.float32)
    return summed


def weight_terms(window, grad_rows):
    groups = []
    for shift_x in range(3):
        stacked = gather_columns(window, shift_x)
        product = jnp.dot(stacked.T, grad_rows, preferred_element_type=jnp.float32)
        groups.append(product.reshape(9, window.shape[-1], grad_rows.shape[1]))
    return jnp.concatenate(groups, axis=0)


def flipped(weight):
    return jnp.transpose(weight[::-1], (0, 2, 1))


def silu_slope(pre_value):
    sigmoid_value = jax.nn.sigmoid(pre_value)
    return sigmoid_value * (1.0 + pre_value * (1.0 - sigmoid_value))


def neighbour_rows(blocks, send_rows):

    def select_face(drift_step, wire_step):
        first_row = segment_start(drift_step, wire_step)
        entries = send_rows[first_row : first_row + segment_length(drift_step, wire_step)]
        return jnp.take(blocks, entries, axis=0)

    arrived = {}
    for drift_step in (-1, 1):
        arrived[drift_step, 0] = from_behind(select_face(-drift_step, 0), "drift", -drift_step)
    for wire_step in (-1, 1):
        arrived[0, wire_step] = from_behind(select_face(0, -wire_step), "wire", -wire_step)
    for drift_step in (-1, 1):
        edge_blocks = jnp.stack([select_face(-drift_step, -1), select_face(-drift_step, 1)])
        shifted = from_behind(edge_blocks, "drift", -drift_step)
        for member, wire_step in ((0, 1), (1, -1)):
            arrived[drift_step, wire_step] = from_behind(shifted[member], "wire", -wire_step)
    return jnp.concatenate([arrived[direction] for direction in DIRECTIONS], axis=0)


def on_device(features, first_weight, second_weight, cotangent, counts, kernel_map, send_lists):
    slot_count = kernel_map.shape[3]
    channels = features.shape[3]
    row_count = slot_count * 64
    kernel_rows = kernel_map[0, 0]
    send_rows = send_lists[0, 0]
    live_rows = (jnp.arange(row_count, dtype=jnp.int32) // 64 < counts[0, 0])[:, None]
    masked_input = jnp.where(live_rows, features[0, 0], jnp.zeros_like(features[0, 0]))
    zero_block = jnp.zeros((1, 4, 4, 4, channels), jnp.bfloat16)

    def window_of(source):
        blocks = jnp.concatenate(
            [source.reshape(slot_count, 4, 4, 4, channels), zero_block], axis=0
        )
        block_table = jnp.concatenate([blocks, neighbour_rows(blocks, send_rows)], axis=0)
        return neighbourhood(block_table, kernel_rows)

    first_window = window_of(masked_input)
    first_pre = convolve(first_window, first_weight)
    hidden = jnp.where(live_rows, jax.nn.silu(first_pre), 0.0).astype(jnp.bfloat16)
    hidden_window = window_of(hidden)
    second_pre = convolve(hidden_window, second_weight)
    output = jnp.where(live_rows, masked_input.astype(jnp.float32) + second_pre, 0.0).astype(
        jnp.bfloat16
    )
    grad_in = jnp.where(live_rows, cotangent[0, 0], jnp.zeros_like(cotangent[0, 0]))
    back_hidden = convolve(window_of(grad_in), flipped(second_weight))
    second_terms = weight_terms(hidden_window, grad_in)
    back_pre = jnp.where(live_rows, back_hidden * silu_slope(first_pre), 0.0).astype(jnp.bfloat16)
    back_input = convolve(window_of(back_pre), flipped(first_weight))
    grad_features = jnp.where(live_rows, grad_in.astype(jnp.float32) + back_input, 0.0).astype(
        jnp.bfloat16
    )
    first_terms = weight_terms(first_window, back_pre)
    first_terms, second_terms = lax.psum((first_terms, second_terms), ("drift", "wire"))
    divisor = math.sqrt(float(lax.axis_size("drift") * lax.axis_size("wire") * row_count))
    return (
        output[None, None],
        grad_features[None, None],
        first_terms / divisor,
        second_terms / divisor,
    )


def solution(mesh):
    placed = (
        P("drift", "wire", None, None),
        P(),
        P(),
        P("drift", "wire", None, None),
        P("drift", "wire"),
        P("drift", "wire", None, None),
        P("drift", "wire", None),
    )
    return jax.shard_map(
        on_device,
        mesh=mesh,
        in_specs=placed,
        out_specs=(P("drift", "wire", None, None), P("drift", "wire", None, None), P(), P()),
        check_vma=False,
    )
```

profile of v0, /device:TPU:1, one launch (start us, length us, event | category | flops | bytes accessed | tf_op | source)
XLA Modules:
  0.0 822.2 jit_solution(13615742205843235736)
XLA Ops:
  12.3 4.6 collective-permute-start.20
  18.9 2.4 collective-permute-start.21
  23.3 3.6 collective-permute-start.22
  39.7 3.9 collective-permute-start.24
  43.6 3.4 slice_reduce_fusion.8
  101.5 2.6 collective-permute-done.27
  107.1 2.1 collective-permute-start.7
  109.2 3.5 collective-permute-done.7
  114.7 2.4 collective-permute-start.1
  118.0 4.3 collective-permute-start.2
  125.2 4.0 collective-permute-start.25
  131.4 4.1 collective-permute-done.26
  135.4 4.8 collective-permute-start.28
  142.5 4.4 collective-permute-done.29
  146.8 4.8 collective-permute-start.5
  153.3 4.3 collective-permute-start.8
  159.2 4.1 collective-permute-done.9
  252.1 2.2 gather_fusion.31
  254.3 2.2 gather_fusion.32
  257.9 2.2 gather_fusion.33
  268.5 9.5 %collective-permute-start.30 = (bf16[3,4,4,4,128]{4,3,2,1,0:T(4,128)(2,1)S(1)}, bf16[3,4,4,4,128]{4,3,2,1,0:T(4,128)(2,1)S(1)}, u32[]{:S(2)}, u32[]{:S(2)}) collective-permute-start(bf16[3,4,4,4,128]{4,3,2,1,0:T(4,128)(2,1)S(1)} %get-tuple-element.388), channel_id=1, source_target_pairs={{0,16},{16,32},{32,48},{48,64},{64,80},{80,96},{96,112},{112,128},... | collective-permute-start | bytes 147464 | tf_op jit(solution)/shard_map/ppermute | solution.py:19
  280.2 3.6 collective-permute-start.32
  285.3 3.9 collective-permute-start.34
  292.7 3.8 collective-permute-done.37
  296.5 3.0 collective-permute-start.14
  302.5 4.9 collective-permute-done.17
  307.3 2.3 collective-permute-start.10
  311.7 5.6 collective-permute-start.12
  318.8 5.5 collective-permute-start.35
  326.4 6.2 collective-permute-done.36
  332.6 4.7 collective-permute-start.38
  339.4 5.5 collective-permute-done.39
  345.0 7.7 collective-permute-start.15
  354.3 4.6 collective-permute-start.18
  360.8 4.2 collective-permute-done.19
  430.1 2.0 gather_fusion.58
  432.1 2.2 gather_fusion.119
  434.4 2.2 gather_fusion.57
  438.0 2.0 gather_fusion.118
  441.5 2.0 gather_fusion.56
  480.5 2.6 copy.944
  483.2 2.9 fusion.11
  488.8 2.9 fusion.13
  494.4 2.1 fusion.15
  512.7 2.5 fusion.9
  518.1 2.5 fusion.10
  520.6 290.1 %all-reduce.7.cloned.1.call-done = (f32[27,128,128]{2,1,0:T(8,128)}, f32[27,128,128]{2,1,0:T(8,128)}) async-done(((f32[27,128,128]{2,1,0:T(8,128)}, f32[27,128,128]{2,1,0:T(8,128)}), (f32[27,128,128]{2,1,0:T(8,128)}, f32[27,128,128]{2,1,0:T(8,128)})) %all-reduce.7.cloned.1.call-update) | async-done | bytes 3538960 | tf_op jit(solution)/shard_map/psum | solution.py:155
  810.7 3.1 broadcast_multiply_fusion.1
  (1057 shorter events, 330.9 us)
Async XLA Ops:
  7.2 803.6 %all-reduce.7.cloned.1.call-start = ((), (), s32[]{:S(2)}) async-start(), calls=%async_computation | async-start | bytes 7077888 | tf_op jit(solution)/shard_map/psum | solution.py:155
  10.2 33.4 %copy-start.5 = (s32[1,1,27,9]{2,1,3,0:T(1,128)S(1)}, s32[1,1,27,9]{2,1,3,0:T(1,128)}, u32[]{:S(2)}) copy-start(s32[1,1,27,9]{2,1,3,0:T(1,128)} %param.32) | copy-start | bytes 2920
  10.3 54.1 %copy-start.3 = (bf16[27,128,128]{2,1,0:T(8,128)(2,1)S(1)}, bf16[27,128,128]{2,1,0:T(8,128)(2,1)}, u32[]{:S(2)}) copy-start(bf16[27,128,128]{2,1,0:T(8,128)(2,1)} %param.29) | copy-start | bytes 2654212
  12.3 102.4 %collective-permute-start.20 = (bf16[3,4,4,4,128]{4,3,2,1,0:T(4,128)(2,1)}, bf16[3,4,4,4,128]{4,3,2,1,0:T(4,128)(2,1)}, u32[]{:S(2)}, u32[]{:S(2)}) collective-permute-start(bf16[3,4,4,4,128]{4,3,2,1,0:T(4,128)(2,1)} %get-tuple-element.442), channel_id=1, source_target_pairs={{0,16},{16,32},{32,48},{48,64},{64,80},{80,96},{96,112},{112,128},... | collective-permute-start | bytes 147464 | tf_op jit(solution)/shard_map/ppermute | solution.py:19
  16.9 46.9 %copy-start.137 = (s32[1024]{0:T(1024)}, s32[1024]{0:T(1024)S(1)}, u32[]{:S(2)}) copy-start(s32[1024]{0:T(1024)S(1)} %pad_clamp_fusion.29) | copy-start | bytes 12292
  18.9 99.1 %collective-permute-start.21 = (bf16[3,4,4,4,128]{4,3,2,1,0:T(4,128)(2,1)}, bf16[3,4,4,4,128]{4,3,2,1,0:T(4,128)(2,1)}, u32[]{:S(2)}, u32[]{:S(2)}) collective-permute-start(bf16[3,4,4,4,128]{4,3,2,1,0:T(4,128)(2,1)} %get-tuple-element.440), channel_id=1, source_target_pairs={{16,0},{32,16},{48,32},{64,48},{80,64},{96,80},{112,96},{128,112},... | collective-permute-start | bytes 147464 | tf_op jit(solution)/shard_map/ppermute | solution.py:19
  21.3 42.5 %copy-start.138 = (s32[1024]{0:T(1024)}, s32[1024]{0:T(1024)S(1)}, u32[]{:S(2)}) copy-start(s32[1024]{0:T(1024)S(1)} %pad_clamp_fusion.28) | copy-start | bytes 12292
  23.3 99.8 %collective-permute-start.22 = (bf16[3,4,4,4,128]{4,3,2,1,0:T(4,128)(2,1)}, bf16[3,4,4,4,128]{4,3,2,1,0:T(4,128)(2,1)}, u32[]{:S(2)}, u32[]{:S(2)}) collective-permute-start(bf16[3,4,4,4,128]{4,3,2,1,0:T(4,128)(2,1)} %get-tuple-element.438), channel_id=1, source_target_pairs={{0,1},{1,2},{2,3},{3,4},{4,5},{5,6},{6,7},{7,8},{8,9},{9,10},{10,1... | collective-permute-start | bytes 147464 | tf_op jit(solution)/shard_map/ppermute | solution.py:19
  26.9 36.9 %copy-start.139 = (s32[1024]{0:T(1024)}, s32[1024]{0:T(1024)S(1)}, u32[]{:S(2)}) copy-start(s32[1024]{0:T(1024)S(1)} %pad_clamp_fusion.27) | copy-start | bytes 12292
  28.9 96.4 %collective-permute-start.23 = (bf16[3,4,4,4,128]{4,3,2,1,0:T(4,128)(2,1)}, bf16[3,4,4,4,128]{4,3,2,1,0:T(4,128)(2,1)}, u32[]{:S(2)}, u32[]{:S(2)}) collective-permute-start(bf16[3,4,4,4,128]{4,3,2,1,0:T(4,128)(2,1)} %get-tuple-element.436), channel_id=1, source_target_pairs={{1,0},{2,1},{3,2},{4,3},{5,4},{6,5},{7,6},{8,7},{9,8},{10,9},{11,1... | collective-permute-start | bytes 147464 | tf_op jit(solution)/shard_map/ppermute | solution.py:19
  39.7 59.1 %collective-permute-start.24 = (bf16[2,1,4,4,4,128]{5,4,3,2,1,0:T(4,128)(2,1)}, bf16[2,1,4,4,4,128]{5,4,3,2,1,0:T(4,128)(2,1)}, u32[]{:S(2)}, u32[]{:S(2)}) collective-permute-start(bf16[2,1,4,4,4,128]{5,4,3,2,1,0:T(4,128)(2,1)} %pad_maximum_fusion.14), channel_id=1, source_target_pairs={{0,16},{16,32},{32,48},{48,64},{64,80},{80,96},{96,112},{112,128},... | collective-permute-start | bytes 98312 | tf_op jit(solution)/shard_map/ppermute | solution.py:19
  97.7 25.4 %copy-start.117 = (bf16[3,4,4,4,128]{4,3,2,1,0:T(4,128)(2,1)S(1)}, bf16[3,4,4,4,128]{4,3,2,1,0:T(4,128)(2,1)}, u32[]{:S(2)}) copy-start(bf16[3,4,4,4,128]{4,3,2,1,0:T(4,128)(2,1)} %get-tuple-element.437) | copy-start | bytes 147460
  98.8 148.8 %copy-start.125 = (pred[576]{0:T(1024)(128)(4,1)}, pred[576]{0:T(1024)(128)(4,1)S(1)}, u32[]{:S(2)}) copy-start(pred[576]{0:T(1024)(128)(4,1)S(1)} %fusion.19) | copy-start | bytes 1732
  98.8 5.2 collective-permute-start.27
  104.0 3.1 collective-permute-start.4
  107.1 5.6 collective-permute-start.7
  112.8 39.2 %collective-permute-start = (bf16[3,4,4,4,128]{4,3,2,1,0:T(4,128)(2,1)S(1)}, bf16[3,4,4,4,128]{4,3,2,1,0:T(4,128)(2,1)S(1)}, u32[]{:S(2)}, u32[]{:S(2)}) collective-permute-start(bf16[3,4,4,4,128]{4,3,2,1,0:T(4,128)(2,1)S(1)} %copy-done.114), channel_id=1, source_target_pairs={{0,16},{16,32},{32,48},{48,64},{64,80},{80,96},{96,112},{112,128},... | collective-permute-start | bytes 147464 | tf_op jit(solution)/shard_map/ppermute | solution.py:19
  114.7 38.6 %collective-permute-start.1 = (bf16[3,4,4,4,128]{4,3,2,1,0:T(4,128)(2,1)S(1)}, bf16[3,4,4,4,128]{4,3,2,1,0:T(4,128)(2,1)S(1)}, u32[]{:S(2)}, u32[]{:S(2)}) collective-permute-start(bf16[3,4,4,4,128]{4,3,2,1,0:T(4,128)(2,1)S(1)} %copy-done.115), channel_id=1, source_target_pairs={{16,0},{32,16},{48,32},{64,48},{80,64},{96,80},{112,96},{128,112},... | collective-permute-start | bytes 147464 | tf_op jit(solution)/shard_map/ppermute | solution.py:19
  118.0 39.6 %collective-permute-start.2 = (bf16[3,4,4,4,128]{4,3,2,1,0:T(4,128)(2,1)S(1)}, bf16[3,4,4,4,128]{4,3,2,1,0:T(4,128)(2,1)S(1)}, u32[]{:S(2)}, u32[]{:S(2)}) collective-permute-start(bf16[3,4,4,4,128]{4,3,2,1,0:T(4,128)(2,1)S(1)} %copy-done.116), channel_id=1, source_target_pairs={{0,1},{1,2},{2,3},{3,4},{4,5},{5,6},{6,7},{7,8},{8,9},{9,10},{10,1... | collective-permute-start | bytes 147464 | tf_op jit(solution)/shard_map/ppermute | solution.py:19
  123.1 36.0 %collective-permute-start.3 = (bf16[3,4,4,4,128]{4,3,2,1,0:T(4,128)(2,1)S(1)}, bf16[3,4,4,4,128]{4,3,2,1,0:T(4,128)(2,1)S(1)}, u32[]{:S(2)}, u32[]{:S(2)}) collective-permute-start(bf16[3,4,4,4,128]{4,3,2,1,0:T(4,128)(2,1)S(1)} %copy-done.117), channel_id=1, source_target_pairs={{1,0},{2,1},{3,2},{4,3},{5,4},{6,5},{7,6},{8,7},{9,8},{10,9},{11,1... | collective-permute-start | bytes 147464 | tf_op jit(solution)/shard_map/ppermute | solution.py:19
  125.2 4.8 collective-permute-start.25
  130.1 5.4 collective-permute-start.26
  135.4 5.7 collective-permute-start.28
  141.1 5.7 collective-permute-start.29
  146.8 12.3 %collective-permute-start.5 = (bf16[1,4,4,4,128]{4,3,2,1,0:T(4,128)(2,1)S(1)}, bf16[1,4,4,4,128]{4,3,2,1,0:T(4,128)(2,1)S(1)}, u32[]{:S(2)}, u32[]{:S(2)}) collective-permute-start(bf16[1,4,4,4,128]{4,3,2,1,0:T(4,128)(2,1)S(1)} %get-tuple-element.325), channel_id=1, source_target_pairs={{0,1},{1,2},{2,3},{3,4},{4,5},{5,6},{6,7},{7,8},{8,9},{9,10},{10,1... | collective-permute-start | bytes 49160 | tf_op jit(solution)/shard_map/ppermute | solution.py:19
  151.9 7.2 collective-permute-start.6
  153.3 5.9 collective-permute-start.8
  157.6 5.7 collective-permute-start.9
  268.5 41.1 %collective-permute-start.30 = (bf16[3,4,4,4,128]{4,3,2,1,0:T(4,128)(2,1)S(1)}, bf16[3,4,4,4,128]{4,3,2,1,0:T(4,128)(2,1)S(1)}, u32[]{:S(2)}, u32[]{:S(2)}) collective-permute-start(bf16[3,4,4,4,128]{4,3,2,1,0:T(4,128)(2,1)S(1)} %get-tuple-element.388), channel_id=1, source_target_pairs={{0,16},{16,32},{32,48},{48,64},{64,80},{80,96},{96,112},{112,128},... | collective-permute-start | bytes 147464 | tf_op jit(solution)/shard_map/ppermute | solution.py:19
  278.2 33.6 %collective-permute-start.31 = (bf16[3,4,4,4,128]{4,3,2,1,0:T(4,128)(2,1)S(1)}, bf16[3,4,4,4,128]{4,3,2,1,0:T(4,128)(2,1)S(1)}, u32[]{:S(2)}, u32[]{:S(2)}) collective-permute-start(bf16[3,4,4,4,128]{4,3,2,1,0:T(4,128)(2,1)S(1)} %get-tuple-element.386), channel_id=1, source_target_pairs={{16,0},{32,16},{48,32},{64,48},{80,64},{96,80},{112,96},{128,112},... | collective-permute-start | bytes 147464 | tf_op jit(solution)/shard_map/ppermute | solution.py:19
  280.2 37.2 %collective-permute-start.32 = (bf16[3,4,4,4,128]{4,3,2,1,0:T(4,128)(2,1)S(1)}, bf16[3,4,4,4,128]{4,3,2,1,0:T(4,128)(2,1)S(1)}, u32[]{:S(2)}, u32[]{:S(2)}) collective-permute-start(bf16[3,4,4,4,128]{4,3,2,1,0:T(4,128)(2,1)S(1)} %get-tuple-element.384), channel_id=1, source_target_pairs={{0,1},{1,2},{2,3},{3,4},{4,5},{5,6},{6,7},{7,8},{8,9},{9,10},{10,1... | collective-permute-start | bytes 147464 | tf_op jit(solution)/shard_map/ppermute | solution.py:19
  284.0 34.7 %collective-permute-start.33 = (bf16[3,4,4,4,128]{4,3,2,1,0:T(4,128)(2,1)S(1)}, bf16[3,4,4,4,128]{4,3,2,1,0:T(4,128)(2,1)S(1)}, u32[]{:S(2)}, u32[]{:S(2)}) collective-permute-start(bf16[3,4,4,4,128]{4,3,2,1,0:T(4,128)(2,1)S(1)} %get-tuple-element.382), channel_id=1, source_target_pairs={{1,0},{2,1},{3,2},{4,3},{5,4},{6,5},{7,6},{8,7},{9,8},{10,9},{11,1... | collective-permute-start | bytes 147464 | tf_op jit(solution)/shard_map/ppermute | solution.py:19
  285.3 5.4 collective-permute-start.34
  290.7 5.8 collective-permute-start.37
  296.5 4.0 collective-permute-start.14
  300.5 6.8 collective-permute-start.17
  307.3 45.6 %collective-permute-start.10 = (bf16[3,4,4,4,128]{4,3,2,1,0:T(4,128)(2,1)S(1)}, bf16[3,4,4,4,128]{4,3,2,1,0:T(4,128)(2,1)S(1)}, u32[]{:S(2)}, u32[]{:S(2)}) collective-permute-start(bf16[3,4,4,4,128]{4,3,2,1,0:T(4,128)(2,1)S(1)} %get-tuple-element.389), channel_id=1, source_target_pairs={{0,16},{16,32},{32,48},{48,64},{64,80},{80,96},{96,112},{112,128},... | collective-permute-start | bytes 147464 | tf_op jit(solution)/shard_map/ppermute | solution.py:19
  309.7 44.6 %collective-permute-start.11 = (bf16[3,4,4,4,128]{4,3,2,1,0:T(4,128)(2,1)S(1)}, bf16[3,4,4,4,128]{4,3,2,1,0:T(4,128)(2,1)S(1)}, u32[]{:S(2)}, u32[]{:S(2)}) collective-permute-start(bf16[3,4,4,4,128]{4,3,2,1,0:T(4,128)(2,1)S(1)} %get-tuple-element.387), channel_id=1, source_target_pairs={{16,0},{32,16},{48,32},{64,48},{80,64},{96,80},{112,96},{128,112},... | collective-permute-start | bytes 147464 | tf_op jit(solution)/shard_map/ppermute | solution.py:19
  311.7 47.2 %collective-permute-start.12 = (bf16[3,4,4,4,128]{4,3,2,1,0:T(4,128)(2,1)S(1)}, bf16[3,4,4,4,128]{4,3,2,1,0:T(4,128)(2,1)S(1)}, u32[]{:S(2)}, u32[]{:S(2)}) collective-permute-start(bf16[3,4,4,4,128]{4,3,2,1,0:T(4,128)(2,1)S(1)} %get-tuple-element.385), channel_id=1, source_target_pairs={{0,1},{1,2},{2,3},{3,4},{4,5},{5,6},{6,7},{7,8},{8,9},{9,10},{10,1... | collective-permute-start | bytes 147464 | tf_op jit(solution)/shard_map/ppermute | solution.py:19
  317.4 43.2 %collective-permute-start.13 = (bf16[3,4,4,4,128]{4,3,2,1,0:T(4,128)(2,1)S(1)}, bf16[3,4,4,4,128]{4,3,2,1,0:T(4,128)(2,1)S(1)}, u32[]{:S(2)}, u32[]{:S(2)}) collective-permute-start(bf16[3,4,4,4,128]{4,3,2,1,0:T(4,128)(2,1)S(1)} %get-tuple-element.383), channel_id=1, source_target_pairs={{1,0},{2,1},{3,2},{4,3},{5,4},{6,5},{7,6},{8,7},{9,8},{10,9},{11,1... | collective-permute-start | bytes 147464 | tf_op jit(solution)/shard_map/ppermute | solution.py:19
  318.8 6.3 collective-permute-start.35
  325.1 7.5 collective-permute-start.36
  332.6 5.6 collective-permute-start.38
  338.1 6.8 collective-permute-start.39
  345.0 15.7 %collective-permute-start.15 = (bf16[1,4,4,4,128]{4,3,2,1,0:T(4,128)(2,1)S(1)}, bf16[1,4,4,4,128]{4,3,2,1,0:T(4,128)(2,1)S(1)}, u32[]{:S(2)}, u32[]{:S(2)}) collective-permute-start(bf16[1,4,4,4,128]{4,3,2,1,0:T(4,128)(2,1)S(1)} %get-tuple-element.321), channel_id=1, source_target_pairs={{0,1},{1,2},{2,3},{3,4},{4,5},{5,6},{6,7},{7,8},{8,9},{9,10},{10,1... | collective-permute-start | bytes 49160 | tf_op jit(solution)/shard_map/ppermute | solution.py:19
  352.9 7.8 collective-permute-start.16
  354.3 6.5 collective-permute-start.18
  358.9 6.0 collective-permute-start.19
  (197 other events, 1512.9 us)
Sparse Core Ops, SparseCore 0:
  508.9 301.7 all-reduce.6
where the time goes:
time: 836 us; the launch traced here: 822 us
  waiting for transfers between devices  338 us (40%)
  local copies, waits for them, and re-layouts  221 us (26%)
  starting transfers between devices  121 us (14%)
  other arithmetic  92 us (11%)
  between operations  27.1 us (3%)
  matrix products  22.7 us (3%)
    psum x1, waiting for transfers between devices, on_device(): lax.psum((first_terms, second_terms), ('drift', 'wire'))  290 us
    ppermute x40, starting transfers between devices, from_behind(): lax.ppermute(value, axis, [(source, source + steps) for source in range(i...  121 us
    gather x108, local copies, waits for them, and re-layouts, neighbourhood(): pieces.append(jnp.take(sliced, kernel_rows[offset], axis=0))  105 us
    unnamed x612, local copies, waits for them, and re-layouts  49 us
    ppermute x40, waiting for transfers between devices, from_behind(): lax.ppermute(value, axis, [(source, source + steps) for source in range(i...  47.9 us
    select_n x72, other arithmetic, neighbourhood(): pieces.append(jnp.take(sliced, kernel_rows[offset], axis=0))  31.4 us
    gather x31, other arithmetic  27.5 us
    gather x16, local copies, waits for them, and re-layouts, select_face(): return jnp.take(blocks, entries, axis=0)  18.5 us
  transfers between devices with their start and end apart: 41, of which 16 were waited for; matrix products, arithmetic and copies ran while one was open for 10% of the time, Pallas kernels for 0%

commit v1 on v0

v1 whole, which is shorter than its diff:
```python
import functools
import math

import jax
import jax.numpy as jnp
from jax import lax
from jax.experimental import pallas as pl
from jax.experimental.pallas import tpu as pltpu
from jax.sharding import PartitionSpec as P

C = 128
PLANES = 12 * 4
ROWS = PLANES * 16
TAPS = 27
MESH = pl.DeviceIdType.MESH
NEIGHBOURS = ((-1, 0), (1, 0), (0, -1), (0, 1), (-1, -1), (-1, 1), (1, -1), (1, 1))


def place(drift, wire):
    return (drift, wire)


def greet(peers):
    barrier = pltpu.get_barrier_semaphore()
    for peer in peers:
        pl.semaphore_signal(barrier, inc=1, device_id=peer, device_id_type=MESH)
    pl.semaphore_wait(barrier, len(peers))


def halo_kernel(sizes, x_ref, y_ref, c_ref, xo_ref, yo_ref, co_ref, send_sem, recv_sem):
    drift_size, wire_size = sizes
    d = lax.axis_index("drift")
    w = lax.axis_index("wire")
    peers = [
        place(
            lax.rem(d + dd + drift_size, drift_size), lax.rem(w + ww + wire_size, wire_size)
        )
        for dd, ww in NEIGHBOURS
    ]
    greet(peers)
    copies = []
    for n, peer in enumerate(peers):
        src, dst, slot = (
            (x_ref, xo_ref, n) if n < 2 else (y_ref, yo_ref, n - 2) if n < 4 else (c_ref, co_ref, n - 4)
        )
        copy = pltpu.make_async_remote_copy(
            src_ref=src.at[slot],
            dst_ref=dst.at[slot],
            send_sem=send_sem.at[n],
            recv_sem=recv_sem.at[n],
            device_id=peer,
            device_id_type=MESH,
        )
        copy.start()
        copies.append(copy)
    for copy in copies:
        copy.wait()


def exchange(fields, sizes, ident):
    x_send = jnp.stack([fields[:, 0], fields[:, 11]])
    y_send = jnp.stack([fields[:, :, :, 1], fields[:, :, :, 12]]).reshape(2, 2 * PLANES, C)
    c_send = jnp.stack(
        [fields[:, x, :, y] for x in (0, 11) for y in (1, 12)]
    ).reshape(4, 8, C)
    vmem = pl.BlockSpec(memory_space=pltpu.VMEM)
    x_got, y_got, c_got = pl.pallas_call(
        functools.partial(halo_kernel, sizes),
        out_shape=[jax.ShapeDtypeStruct(a.shape, a.dtype) for a in (x_send, y_send, c_send)],
        in_specs=[vmem] * 3,
        out_specs=[vmem] * 3,
        scratch_shapes=[pltpu.SemaphoreType.DMA((8,)), pltpu.SemaphoreType.DMA((8,))],
        compiler_params=pltpu.CompilerParams(collective_id=ident, has_side_effects=True),
        name="halo" + str(ident),
    )(x_send, y_send, c_send)
    d = lax.axis_index("drift")
    w = lax.axis_index("wire")
    d_low, d_high = d > 0, d < sizes[0] - 1
    w_low, w_high = w > 0, w < sizes[1] - 1

    def keep(value, ok):
        return jnp.where(ok, value, jnp.zeros_like(value))

    x_low = keep(x_got[1], d_low)[:, None]
    x_high = keep(x_got[0], d_high)[:, None]
    y_got = y_got.reshape(2, 2, 12, 4, C)
    c_got = c_got.reshape(4, 2, 1, 4, C)
    y_low = jnp.concatenate(
        [keep(c_got[3], d_low & w_low), keep(y_got[1], w_low), keep(c_got[1], d_high & w_low)], axis=1
    )
    y_high = jnp.concatenate(
        [keep(c_got[2], d_low & w_high), keep(y_got[0], w_high), keep(c_got[0], d_high & w_high)], axis=1
    )
    base = jnp.concatenate([x_low, fields, x_high], axis=1)
    rows = lax.broadcasted_iota(jnp.int32, base.shape, 3)
    return jnp.where(
        rows == 0, y_low[:, :, :, None], jnp.where(rows == 13, y_high[:, :, :, None], base)
    )


def columns(source, padded, shifted, out):
    padded[...] = jnp.zeros_like(padded)
    for x in range(14):
        start = 8 + (x * 6 + 1) * 16
        padded[start : start + 64, :] = source[x].reshape(64, C).astype(jnp.float32)
    for oy in range(3):
        shifted[...] = padded[7 + oy : 7 + oy + 1344, :].astype(jnp.bfloat16).reshape(14, 96, C)
        for ox in range(3):
            for oz in range(3):
                k = 9 * ox + 3 * oy + oz
                out[:, k * C : (k + 1) * C] = shifted[
                    ox : ox + 12, oz * 16 : oz * 16 + 64, :
                ].reshape(ROWS, C)


def first_kernel(
    pad_ref, w1_ref, w2f_ref, mask_ref, hid_ref, bp_ref, g_ref,
    padded, shifted, cols_m, cols_g, hid_t, bp_t,
):
    columns(pad_ref.at[0], padded, shifted, cols_m)
    columns(pad_ref.at[1], padded, shifted, cols_g)

    def rows_step(i, carry):
        rows = pl.ds(pl.multiple_of(i * 256, 256), 256)
        pre = jnp.dot(cols_m[rows, :], w1_ref[...], preferred_element_type=jnp.float32)
        back = jnp.dot(cols_g[rows, :], w2f_ref[...], preferred_element_type=jnp.float32)
        live = mask_ref[rows, :] > 0
        gate = 1.0 / (1.0 + jnp.exp(-pre))
        hid = jnp.where(live, pre / (1.0 + jnp.exp(-pre)), 0.0)
        bp = jnp.where(live, back * (gate * (1.0 + pre * (1.0 - gate))), 0.0)
        hid_ref[rows, :] = hid.astype(jnp.bfloat16)
        bp_ref[rows, :] = bp.astype(jnp.bfloat16)
        hid_t[:, rows] = hid.T.astype(jnp.bfloat16)
        bp_t[:, rows] = bp.T.astype(jnp.bfloat16)
        return carry

    lax.fori_loop(0, ROWS // 256, rows_step, 0)

    def taps_step(j, carry):
        lanes = pl.ds(pl.multiple_of(j * 3 * C, C), 3 * C)
        one = jnp.dot(bp_t[...], cols_m[:, lanes], preferred_element_type=jnp.float32)
        two = jnp.dot(hid_t[...], cols_g[:, lanes], preferred_element_type=jnp.float32)
        for t in range(3):
            k = 3 * j + t
            part = slice(t * C, (t + 1) * C)
            g_ref[0, pl.ds(pl.multiple_of(k * C, C), C), :] = one[:, part].T
            g_ref[1, pl.ds(pl.multiple_of((26 - k) * C, C), C), :] = two[:, part]
        return carry

    lax.fori_loop(0, 9, taps_step, 0)


def second_kernel(
    pad_ref, w2_ref, w1f_ref, own_ref, out_ref, padded, shifted, cols
):
    for field, weight in ((0, w2_ref), (1, w1f_ref)):
        columns(pad_ref.at[field], padded, shifted, cols)

        def rows_step(i, carry):
            rows = pl.ds(pl.multiple_of(i * 256, 256), 256)
            value = jnp.dot(cols[rows, :], weight[...], preferred_element_type=jnp.float32)
            out_ref[field, rows, :] = (own_ref[field, rows, :].astype(jnp.float32) + value).astype(
                jnp.bfloat16
            )
            return carry

        lax.fori_loop(0, ROWS // 256, rows_step, 0)


def reduce_kernel(
    sizes, scale, g_ref, o_ref, pair_in, chip_out, chip_in, acc, wire_in, gathered,
    pair_s, pair_r, chip_s, chip_r, wire_s, wire_r, back_s, back_r, out_s, out_r, fwd_s, fwd_r,
):
    drift_size, wire_size = sizes
    chips = drift_size // 2
    chunk = TAPS * C // chips
    piece = acc.shape[0] // wire_size
    d = lax.axis_index("drift")
    w = lax.axis_index("wire")
    core = lax.rem(d, 2)
    chip = d // 2
    partner = place(d + 1 - 2 * core, w)
    chip_peers = []
    wire_peers = []
    for i in range(chips):
        chip_peers.append(lax.rem(chip + 1 + i, chips))
    for i in range(wire_size - 1):
        wire_peers.append(lax.rem(w + 1 + i, wire_size))
    chip_places = [place(2 * peer + core, w) for peer in chip_peers[:-1]]
    wire_places = [place(d, peer) for peer in wire_peers]
    greet([partner] + chip_places + wire_places)

    def send(src, dst, send_sem, recv_sem, peer):
        copy = pltpu.make_async_remote_copy(
            src_ref=src, dst_ref=dst, send_sem=send_sem, recv_sem=recv_sem,
            device_id=peer, device_id_type=MESH,
        )
        copy.start()
        return copy

    def span(index, size):
        return pl.ds(pl.multiple_of(index * size, 16), size)

    pair = []
    for i, peer in enumerate(chip_peers):
        pair.append(
            send(
                g_ref.at[1 - core, span(peer, chunk)], pair_in.at[i],
                pair_s.at[i], pair_r.at[i], partner,
            )
        )
    acc[...] = jnp.zeros_like(acc)
    ring = []
    for i, peer in enumerate(chip_peers):
        pair[i].wait_recv()
        total = g_ref[core, span(peer, chunk), :] + pair_in[i]
        if i < chips - 1:
            chip_out[i] = total.astype(jnp.bfloat16)
            ring.append(
                send(chip_out.at[i], chip_in.at[i], chip_s.at[i], chip_r.at[i], chip_places[i])
            )
        else:
            acc[0:chunk, :] = total
    for i, copy in enumerate(ring):
        copy.wait_recv()
        acc[0:chunk, :] += chip_in[i].astype(jnp.float32)
    wires = []
    for i, peer in enumerate(wire_peers):
        wires.append(
            send(
                acc.at[span(peer, piece)], wire_in.at[i], wire_s.at[i], wire_r.at[i],
                wire_places[i],
            )
        )
    own = acc[span(w, piece), :]
    for i, copy in enumerate(wires):
        copy.wait_recv()
        own = own + wire_in[i]
    gathered[span(w, piece), :] = (own * scale).astype(jnp.bfloat16)
    back = []
    for i in range(wire_size - 1):
        mine = gathered.at[span(w, piece)]
        back.append(send(mine, mine, back_s.at[i], back_r.at[i], wire_places[i]))
    for copy in back:
        copy.wait_recv()
    full = gathered.at[0:chunk]
    spot = o_ref.at[core, span(chip, chunk)]
    outs = []
    for i in range(chips - 1):
        outs.append(send(full, spot, out_s.at[i], out_r.at[i], chip_places[i]))
    forwards = [send(full, spot, fwd_s.at[chips - 1], fwd_r.at[chips - 1], partner)]
    o_ref[core, span(chip, chunk), :] = gathered[0:chunk, :]
    for i in range(chips - 1):
        outs[i].wait_recv()
        source = lax.rem(chip + 2 * chips - 1 - i, chips)
        part = o_ref.at[core, span(source, chunk)]
        forwards.append(send(part, part, fwd_s.at[i], fwd_r.at[i], partner))
    for copy in forwards:
        copy.wait_recv()
    for copy in pair + ring + wires + back + outs + forwards:
        copy.wait_send()


def reduce_all(grads, sizes, scale):
    drift_size, wire_size = sizes
    chips = drift_size // 2
    chunk = TAPS * C // chips
    piece = -(-chunk // (wire_size * 16)) * 16
    vmem = pl.BlockSpec(memory_space=pltpu.VMEM)
    dma = pltpu.SemaphoreType.DMA
    return pl.pallas_call(
        functools.partial(reduce_kernel, sizes, scale),
        out_shape=jax.ShapeDtypeStruct((2, TAPS * C, C), jnp.bfloat16),
        in_specs=[vmem],
        out_specs=vmem,
        scratch_shapes=[
            pltpu.VMEM((chips, chunk, C), jnp.float32),
            pltpu.VMEM((chips - 1, chunk, C), jnp.bfloat16),
            pltpu.VMEM((chips - 1, chunk, C), jnp.bfloat16),
            pltpu.VMEM((piece * wire_size, C), jnp.float32),
            pltpu.VMEM((wire_size - 1, piece, C), jnp.float32),
            pltpu.VMEM((piece * wire_size, C), jnp.bfloat16),
            dma((chips,)), dma((chips,)),
            dma((chips - 1,)), dma((chips - 1,)),
            dma((wire_size - 1,)), dma((wire_size - 1,)),
            dma((wire_size - 1,)), dma((wire_size - 1,)),
            dma((chips - 1,)), dma((chips - 1,)),
            dma((chips,)), dma((chips,)),
        ],
        compiler_params=pltpu.CompilerParams(collective_id=2, has_side_effects=True),
        name="reduce",
    )(grads)


def flipped(weight):
    return jnp.transpose(weight[::-1], (0, 2, 1)).reshape(TAPS * C, C)


def on_device(features, first_weight, second_weight, cotangent, counts, kernel_map, send_lists):
    sizes = (lax.axis_size("drift"), lax.axis_size("wire"))
    lists = send_lists[0, 0]
    count = counts[0, 0]
    around = jnp.stack([lists[n] for n in (0, 1, 2, 7, 10, 3, 4, 5)])
    active_around = around < 9
    centre = jnp.where(
        count > jnp.sum(active_around.astype(jnp.int32)),
        jnp.sum(active_around[:4].astype(jnp.int32)),
        9,
    )
    slots = jnp.concatenate([around[:4], centre[None], around[4:]])
    live_pos = slots < 9

    both = jnp.stack([features[0, 0], cotangent[0, 0]]).reshape(2, 9, 64, C)
    picked = jnp.take(both, jnp.minimum(slots, 8), axis=1)
    picked = jnp.where(live_pos[None, :, None, None], picked, jnp.zeros_like(picked))
    dense = picked.reshape(2, 3, 3, 4, 4, 4, C).transpose(0, 1, 3, 5, 2, 4, 6)
    dense = jnp.pad(dense.reshape(2, 12, 4, 12, C), ((0, 0), (0, 0), (0, 0), (1, 3), (0, 0)))

    mask = jnp.broadcast_to(live_pos.reshape(3, 1, 1, 3, 1, 1), (3, 4, 4, 3, 4, C))
    mask = jnp.pad(
        mask.astype(jnp.float32).reshape(12, 4, 12, C), ((0, 0), (0, 0), (1, 3), (0, 0))
    ).reshape(ROWS, C)

    vmem = pl.BlockSpec(memory_space=pltpu.VMEM)
    work = [pltpu.VMEM((1360, C), jnp.float32), pltpu.VMEM((14, 96, C), jnp.bfloat16)]
    cols = pltpu.VMEM((ROWS, TAPS * C), jnp.bfloat16)
    first_padded = exchange(dense, sizes, 0)
    hidden, back_pre, grads = pl.pallas_call(
        first_kernel,
        out_shape=[
            jax.ShapeDtypeStruct((ROWS, C), jnp.bfloat16),
            jax.ShapeDtypeStruct((ROWS, C), jnp.bfloat16),
            jax.ShapeDtypeStruct((2, TAPS * C, C), jnp.float32),
        ],
        in_specs=[vmem] * 4,
        out_specs=[vmem] * 3,
        scratch_shapes=work
        + [cols, cols, pltpu.VMEM((C, ROWS), jnp.bfloat16), pltpu.VMEM((C, ROWS), jnp.bfloat16)],
        compiler_params=pltpu.CompilerParams(vmem_limit_bytes=48 << 20),
        name="first",
    )(first_padded, first_weight.reshape(TAPS * C, C), flipped(second_weight), mask)

    second_padded = exchange(
        jnp.stack([hidden, back_pre]).reshape(2, 12, 4, 16, C), sizes, 1
    )
    summed = pl.pallas_call(
        second_kernel,
        out_shape=jax.ShapeDtypeStruct((2, ROWS, C), jnp.bfloat16),
        in_specs=[vmem] * 4,
        out_specs=vmem,
        scratch_shapes=work + [cols],
        compiler_params=pltpu.CompilerParams(vmem_limit_bytes=32 << 20),
        name="second",
    )(
        second_padded,
        second_weight.reshape(TAPS * C, C),
        flipped(first_weight),
        dense.reshape(2, ROWS, C),
    )
    scale = 1.0 / math.sqrt(float(sizes[0] * sizes[1] * 576))
    reduced = reduce_all(grads, sizes, scale)

    blocks = summed.reshape(2, 3, 4, 4, 16, C)[:, :, :, :, 1:13]
    blocks = blocks.reshape(2, 3, 4, 4, 3, 4, C).transpose(0, 1, 4, 2, 5, 3, 6)
    blocks = blocks.reshape(2, 9, 64, C)
    slot_ids = jnp.arange(9, dtype=jnp.int32)
    matches = slots[None, :] == slot_ids[:, None]
    positions = jnp.sum(jnp.where(matches, slot_ids[None, :], 0), axis=1)
    placed = jnp.take(blocks, positions, axis=1)
    placed = jnp.where((slot_ids < count)[None, :, None, None], placed, jnp.zeros_like(placed))
    placed = placed.reshape(2, 1, 1, 576, C)
    weights = reduced.astype(jnp.float32).reshape(2, TAPS, C, C)
    return placed[0], placed[1], weights[0], weights[1]


def solution(mesh):
    placed = (
        P("drift", "wire", None, None),
        P(),
        P(),
        P("drift", "wire", None, None),
        P("drift", "wire"),
        P("drift", "wire", None, None),
        P("drift", "wire", None),
    )
    return jax.shard_map(
        on_device,
        mesh=mesh,
        in_specs=placed,
        out_specs=(P("drift", "wire", None, None), P("drift", "wire", None, None), P(), P()),
        check_vma=False,
    )
```

time: 836 us -> 138 us (0.17); the launches traced: 822 us -> 137 us
  waiting for transfers between devices: 338 us -> 0 us
  local copies, waits for them, and re-layouts: 221 us -> 27.1 us
  starting transfers between devices: 121 us -> 0 us
  Pallas kernels: 0 us -> 94.8 us
  other arithmetic: 92 us -> 12.2 us
  between operations: 27.1 us -> 2.84 us
  matrix products: 22.7 us -> 0 us
    psum x1 -> x0, waiting for transfers between devices: 290 us -> none  [on_device(): lax.psum((first_terms, second_terms), ('drift', 'wire'))]
    gather x124 -> x2, local copies, waits for them, and re-layouts: 123 us -> 1.21 us  [the longest x1 0.6 us: on_device(): picked = jnp.take(both, jnp.minimum(slots, 8), axis=1)]
    ppermute x40 -> x0, starting transfers between devices: 121 us -> none  [from_behind(): lax.ppermute(value, axis, [(source, source + steps) for source in range(i...]
    pallas_call x0 -> x5, Pallas kernels: none -> 94.8 us  [the longest x1 52.9 us: reduce_all(): pl.pallas_call(functools.partial(reduce_kernel, sizes, scale), out_shape=...]
    ppermute x40 -> x0, waiting for transfers between devices: 47.9 us -> none  [from_behind(): lax.ppermute(value, axis, [(source, source + steps) for source in range(i...]
    unnamed x612 -> x15, local copies, waits for them, and re-layouts: 49 us -> 2.17 us
    select_n x80 -> x11, other arithmetic: 34.8 us -> 5.81 us  [the longest x6 4.49 us: keep(): return jnp.where(ok, value, jnp.zeros_like(value))]
    gather x31 -> x2, other arithmetic: 27.5 us -> 0.01 us
  transfers between devices with their start and end apart: 41 -> 0, of which waited for: 16 -> 0; matrix products, arithmetic and copies ran while one was open for 10% -> 0% of each run, Pallas kernels for 0% -> 0%
where the time goes in v1:
time: 138 us; the launch traced here: 137 us
  Pallas kernels  94.8 us (69%)
  local copies, waits for them, and re-layouts  27.1 us (20%)
  other arithmetic  12.2 us (9%)
  between operations  2.84 us (2%)
    pallas_call x1, Pallas kernels, reduce_all(): pl.pallas_call(functools.partial(reduce_kernel, sizes, scale), out_shape=...  52.9 us
    pallas_call x2, Pallas kernels, exchange(): pl.pallas_call(functools.partial(halo_kernel, sizes), out_shape=[jax.Shap...  26.2 us
    pallas_call x1, Pallas kernels, on_device(): pl.pallas_call(first_kernel, out_shape=[jax.ShapeDtypeStruct((ROWS, C), j...  10.3 us
    transpose x4, local copies, waits for them, and re-layouts, flipped(): return jnp.transpose(weight[::-1], (0, 2, 1)).reshape(TAPS * C, C)  5.78 us
    pallas_call x1, Pallas kernels, on_device(): pl.pallas_call(second_kernel, out_shape=jax.ShapeDtypeStruct((2, ROWS, C)...  5.38 us
    concatenate x1, local copies, waits for them, and re-layouts, on_device(): slots = jnp.concatenate([around[:4], centre[None], around[4:]])  5.15 us
    another operation x1, local copies, waits for them, and re-layouts, on_device(): around = jnp.stack([lists[n] for n in (0, 1, 2, 7, 10, 3, 4, 5)])  5.15 us
    select_n x6, other arithmetic, keep(): return jnp.where(ok, value, jnp.zeros_like(value))  4.49 us

profile of v1, /device:TPU:1, one launch (start us, length us, event | category | flops | bytes accessed | tf_op | source)
XLA Modules:
  0.0 137.0 jit_solution(1293248086606669922)
XLA Ops:
  0.6 1.6 %fusion.8 = (s32[1,1,1]{2,1,0:T(1,128)}, s32[1,1,1]{2,1,0:T(1,128)}, s32[1,1,1]{2,1,0:T(1,128)}, s32[1,1,1]{2,1,0:T(1,128)}, s32[1,1,1]{2,1,0:T(1,128)}, /*index...) fusion(s32[1,1,16]{2,1,0:T(1,128)} %param.14), kind=kLoop, calls=%fused_computation.68 | loop fusion | bytes 64 | tf_op jit(solution)/shard_map/slice | solution.py:303
  2.2 5.1 %stack.61 = s32[8]{0:T(128)S(1)} concatenate(s32[1]{0:T(128)} %bitcast.1, s32[1]{0:T(128)} %bitcast.2, s32[1]{0:T(128)} %bitcast.3, s32[1]{0:T(128)} %bitcast.4, s32[1]{0:T(128)} %bitcast.5, s32[1]{0:T(128)} %bitcast.6, s32[1]{0:T(128)} %bitcast.7, s32[1]{0:T(128)} %bitcast.8), dimensions={0} | concatenate | bytes 64 | tf_op jit(solution)/shard_map/stack | solution.py:303
  7.4 0.7 convert_reduce_fusion
  9.3 0.6 fusion.2
  10.6 5.1 %concatenate.38 = s32[9]{0:T(128)S(1)} concatenate(s32[1]{0:T(128)} %bitcast.1, s32[1]{0:T(128)} %bitcast.2, s32[1]{0:T(128)} %bitcast.3, s32[1]{0:T(128)} %bitcast.4, s32[1]{0:T(128)} %bitcast.9, s32[1]{0:T(128)} %bitcast.5, s32[1]{0:T(128)} %bitcast.6, s32[1]{0:T(128)} %bitcast.7, s32[1]{0:T(128)} %bitcast.8), dimensions={0} | concatenate | bytes 72 | tf_op jit(solution)/shard_map/concatenate | solution.py:310
  15.8 1.0 pad_maximum_fusion
  16.8 0.6 gather_fusion
  17.4 0.1 bitcast_select_fusion.1
  17.6 0.1 copy.46
  17.7 0.6 pad_maximum_fusion.11.c_ref
  18.3 0.6 pad_maximum_fusion.5.y_ref
  18.9 0.1 copy.47
  19.1 0.6 pad_maximum_fusion.1.x_ref
  19.7 16.5 %halo0.1 = (bf16[2,2,4,16,128]{4,3,2,1,0:T(8,128)(2,1)}, bf16[2,96,128]{2,1,0:T(8,128)(2,1)}, bf16[4,8,128]{2,1,0:T(8,128)(2,1)}) custom-call(bf16[2,2,4,16,128]{4,3,2,1,0:T(8,128)(2,1)} %pad_maximum_fusion.1.x_ref, bf16[2,96,128]{2,1,0:T(8,128)(2,1)} %pad_maximum_fusion.5.y_ref, bf16[4,8,128]{2,1,0:T(8,128)(2,1)} %pad_maximum_fusion.11.c_ref), custom_call_target="tpu_custom_call" | custom-call | tf_op jit(solution)/shard_map/halo0/pallas_call | solution.py:67
  36.2 0.8 slice_select_fusion.3
  37.0 0.7 slice_select_fusion.11
  37.7 0.8 select_bitcast_fusion.3
  38.5 0.1 pad.8
  38.7 0.9 fusion.pad_ref
  39.8 0.1 broadcast_in_dim.85
  39.9 0.1 broadcast_in_dim.86
  40.0 0.8 pad.9
  40.8 1.0 reverse_bitcast_fusion.1
  41.8 1.9 %copy.55 = bf16[27,128,128]{2,1,0:T(8,128)(2,1)S(1)} copy(bf16[27,128,128]{1,2,0:T(8,128)(2,1)} %reverse_bitcast_fusion.1) | data formatting | bytes 1769472 | tf_op jit(solution)/shard_map/transpose | solution.py:296
  43.7 1.0 copy-done.2
  44.7 1.0 copy-done.3
  45.7 10.3 %first.1 = (bf16[768,128]{1,0:T(8,128)(2,1)S(1)}, bf16[768,128]{1,0:T(8,128)(2,1)S(1)}, f32[2,3456,128]{2,1,0:T(8,128)}) custom-call(bf16[2,14,4,16,128]{4,3,2,1,0:T(8,128)(2,1)S(1)} %copy-done.2, bf16[3456,128]{1,0:T(8,128)(2,1)S(1)} %bitcast.109, bf16[3456,128]{1,0:T(8,128)(2,1)S(1)} %bitcast.111, f32[768,128]{1,0:T(8,128)S(1)} %bitcast.122), custom_call_target="tpu_custom_call" | custom-call | tf_op jit(solution)/shard_map/first/pallas_call | solution.py:328
  56.0 52.9 %reduce.1 = bf16[2,3456,128]{2,1,0:T(8,128)(2,1)} custom-call(f32[2,3456,128]{2,1,0:T(8,128)} %get-tuple-element.22.g_ref), custom_call_target="tpu_custom_call" | custom-call | tf_op jit(solution)/shard_map/reduce/pallas_call | solution.py:271
  109.0 3.5 %fusion.4 = (f32[1,3456,128]{2,1,0:T(8,128)}, f32[1,3456,128]{2,1,0:T(8,128)}) fusion(bf16[2,3456,128]{2,1,0:T(8,128)(2,1)} %reduce.1), kind=kLoop, calls=%fused_computation.64 | loop fusion | bytes 7077888 | tf_op jit(solution)/shard_map/slice | solution.py:373
  112.5 0.6 pad_maximum_fusion.12.c_ref
  113.1 0.1 pad_maximum_fusion.4
  113.2 0.6 pad_maximum_fusion.6.y_ref
  113.9 0.6 pad_maximum_fusion.2.x_ref
  114.5 9.7 %halo1.1 = (bf16[2,2,4,16,128]{4,3,2,1,0:T(8,128)(2,1)}, bf16[2,96,128]{2,1,0:T(8,128)(2,1)}, bf16[4,8,128]{2,1,0:T(8,128)(2,1)}) custom-call(bf16[2,2,4,16,128]{4,3,2,1,0:T(8,128)(2,1)} %pad_maximum_fusion.2.x_ref, bf16[2,96,128]{2,1,0:T(8,128)(2,1)} %pad_maximum_fusion.6.y_ref, bf16[4,8,128]{2,1,0:T(8,128)(2,1)} %pad_maximum_fusion.12.c_ref), custom_call_target="tpu_custom_call" | custom-call | tf_op jit(solution)/shard_map/halo1/pallas_call | solution.py:67
  124.2 0.8 slice_select_fusion.1
  125.0 0.7 slice_select_fusion.7
  125.7 0.8 select_bitcast_fusion.1
  126.5 0.2 fusion.1.pad_ref
  126.7 1.0 reverse_bitcast_fusion
  127.7 1.9 %copy.62 = bf16[27,128,128]{2,1,0:T(8,128)(2,1)S(1)} copy(bf16[27,128,128]{1,2,0:T(8,128)(2,1)} %reverse_bitcast_fusion) | data formatting | bytes 1769472 | tf_op jit(solution)/shard_map/transpose | solution.py:296
  129.6 5.4 %second.1 = bf16[2,768,128]{2,1,0:T(8,128)(2,1)S(1)} custom-call(bf16[2,14,4,16,128]{4,3,2,1,0:T(8,128)(2,1)S(1)} %fusion.1.pad_ref, bf16[3456,128]{1,0:T(8,128)(2,1)S(1)} %bitcast.110, bf16[3456,128]{1,0:T(8,128)(2,1)S(1)} %bitcast.112, bf16[2,768,128]{2,1,0:T(8,128)(2,1)S(1)} %bitcast.113), custom_call_target="tpu_custom_call" | custom-call | tf_op jit(solution)/shard_map/second/pallas_call | solution.py:346
  135.0 0.1 slice.252
  135.1 0.1 copy.73
  135.3 0.1 copy.64
  135.4 0.1 select_reduce_fusion
  135.5 0.6 gather_fusion.1
  136.2 0.1 bitcast_select_fusion
  136.3 0.7 fusion.5
  (30 shorter events, 0.5 us)
Async XLA Ops:
  19.7 21.0 %copy-start.1 = (bf16[27,128,128]{2,1,0:T(8,128)(2,1)S(1)}, bf16[27,128,128]{2,1,0:T(8,128)(2,1)}, u32[]{:S(2)}) copy-start(bf16[27,128,128]{2,1,0:T(8,128)(2,1)} %param.11) | copy-start | bytes 2654212
  40.8 2.9 %copy-start = (bf16[27,128,128]{2,1,0:T(8,128)(2,1)S(1)}, bf16[27,128,128]{2,1,0:T(8,128)(2,1)}, u32[]{:S(2)}) copy-start(bf16[27,128,128]{2,1,0:T(8,128)(2,1)} %param.10) | copy-start | bytes 2654212
  43.7 1.0 copy-start.2
  44.7 1.0 copy-start.3

commit v2 on v1

v2 whole, which is shorter than its diff:
```python
import functools
import math

import jax
import jax.numpy as jnp
import numpy as np
from jax import lax
from jax.experimental import pallas as pl
from jax.experimental.pallas import tpu as pltpu
from jax.sharding import PartitionSpec as P

C = 128
PLANES = 12 * 4
ROWS = PLANES * 16
TAPS = 27
LISTED = np.arange(16)[None, :] == np.array([0, 1, 2, 7, -1, 10, 3, 4, 5])[:, None]
AROUND = np.arange(9) != 4
BEFORE = np.arange(9) < 4
MESH = pl.DeviceIdType.MESH
NEIGHBOURS = ((-1, 0), (1, 0), (0, -1), (0, 1), (-1, -1), (-1, 1), (1, -1), (1, 1))


def place(drift, wire):
    return (drift, wire)


def greet(peers):
    barrier = pltpu.get_barrier_semaphore()
    for peer in peers:
        pl.semaphore_signal(barrier, inc=1, device_id=peer, device_id_type=MESH)
    pl.semaphore_wait(barrier, len(peers))


def halo_peers(sizes):
    d = lax.axis_index("drift")
    w = lax.axis_index("wire")
    return [
        place(lax.rem(d + dd + sizes[0], sizes[0]), lax.rem(w + ww + sizes[1], sizes[1]))
        for dd, ww in NEIGHBOURS
    ]


def halo_start(peers, sends, halos, send_sem, recv_sem):
    copies = []
    for n, peer in enumerate(peers):
        which, slot = (0, n) if n < 2 else (1, n - 2) if n < 4 else (2, n - 4)
        copy = pltpu.make_async_remote_copy(
            src_ref=sends[which].at[slot],
            dst_ref=halos[which].at[slot],
            send_sem=send_sem.at[n],
            recv_sem=recv_sem.at[n],
            device_id=peer,
            device_id_type=MESH,
        )
        copy.start()
        copies.append(copy)
    return copies


def halo_scratch():
    return [
        pltpu.VMEM((2, 2, 4, 16, C), jnp.bfloat16),
        pltpu.VMEM((2, 2 * PLANES, C), jnp.bfloat16),
        pltpu.VMEM((4, 8, C), jnp.bfloat16),
        pltpu.SemaphoreType.DMA((8,)),
        pltpu.SemaphoreType.DMA((8,)),
    ]


def faces(fields):
    x_send = jnp.stack([fields[:, 0], fields[:, 11]])
    y_send = jnp.stack([fields[:, :, :, 1], fields[:, :, :, 12]]).reshape(2, 2 * PLANES, C)
    c_send = jnp.stack(
        [fields[:, x, :, y] for x in (0, 11) for y in (1, 12)]
    ).reshape(4, 8, C)
    return x_send, y_send, c_send


def flip(weight, out):
    for k in range(TAPS):
        tap = weight[(26 - k) * C : (27 - k) * C, :].astype(jnp.float32)
        out[k * C : (k + 1) * C, :] = tap.T.astype(jnp.bfloat16)


def columns(sizes, field, own, halos, padded, edge, shifted, out):
    x_got, y_got, c_got = halos
    d = lax.axis_index("drift")
    w = lax.axis_index("wire")
    d_ok = (d > 0, d < sizes[0] - 1)
    w_ok = (w > 0, w < sizes[1] - 1)

    def keep(value, ok):
        value = value.astype(jnp.float32)
        return jnp.where(ok, value, jnp.zeros_like(value))

    padded[...] = jnp.zeros_like(padded)
    for x in range(14):
        start = 8 + (x * 6 + 1) * 16
        if x == 0:
            value = keep(x_got[1, field].reshape(64, C), d_ok[0])
        elif x == 13:
            value = keep(x_got[0, field].reshape(64, C), d_ok[1])
        else:
            value = own[field, (x - 1) * 64 : x * 64, :].astype(jnp.float32)
        padded[start : start + 64, :] = value
    for side in range(2):
        edge[0:96, :] = keep(y_got[1 - side], w_ok[side])
        edge[96:104, :] = keep(c_got[3 - side], d_ok[0] & w_ok[side])
        edge[104:112, :] = keep(c_got[1 - side], d_ok[1] & w_ok[side])
        for x in range(14):
            first = 96 if x == 0 else 104 if x == 13 else field * PLANES + (x - 1) * 4
            first = first + (field * 4 if x in (0, 13) else 0)
            start = 8 + (x * 6 + 1) * 16 + 13 * side
            padded[pl.ds(start, 4, stride=16), :] = edge[first : first + 4, :]
    for oy in range(3):
        shifted[...] = padded[7 + oy : 7 + oy + 1344, :].astype(jnp.bfloat16).reshape(14, 96, C)
        for ox in range(3):
            for oz in range(3):
                k = 9 * ox + 3 * oy + oz
                out[:, k * C : (k + 1) * C] = shifted[
                    ox : ox + 12, oz * 16 : oz * 16 + 64, :
                ].reshape(ROWS, C)


def first_kernel(
    sizes, own_ref, x_ref, y_ref, c_ref, w1_ref, w2_ref, mask_ref, mid_ref, g_ref,
    x_got, y_got, c_got, halo_s, halo_r, padded, edge, shifted, w2f, cols_m, cols_g, hid_t, bp_t,
):
    halos = (x_got, y_got, c_got)
    peers = halo_peers(sizes)
    greet(peers)
    copies = halo_start(peers, (x_ref, y_ref, c_ref), halos, halo_s, halo_r)
    flip(w2_ref, w2f)
    for copy in copies:
        copy.wait()
    columns(sizes, 0, own_ref, halos, padded, edge, shifted, cols_m)
    columns(sizes, 1, own_ref, halos, padded, edge, shifted, cols_g)

    def rows_step(i, carry):
        rows = pl.ds(pl.multiple_of(i * 256, 256), 256)
        pre = jnp.dot(cols_m[rows, :], w1_ref[...], preferred_element_type=jnp.float32)
        back = jnp.dot(cols_g[rows, :], w2f[...], preferred_element_type=jnp.float32)
        live = mask_ref[rows, :] > 0
        gate = 1.0 / (1.0 + jnp.exp(-pre))
        hid = jnp.where(live, pre / (1.0 + jnp.exp(-pre)), 0.0)
        bp = jnp.where(live, back * (gate * (1.0 + pre * (1.0 - gate))), 0.0)
        mid_ref[0, rows, :] = hid.astype(jnp.bfloat16)
        mid_ref[1, rows, :] = bp.astype(jnp.bfloat16)
        hid_t[:, rows] = hid.T.astype(jnp.bfloat16)
        bp_t[:, rows] = bp.T.astype(jnp.bfloat16)
        return carry

    lax.fori_loop(0, ROWS // 256, rows_step, 0)

    def taps_step(j, carry):
        lanes = pl.ds(pl.multiple_of(j * 3 * C, C), 3 * C)
        one = jnp.dot(bp_t[...], cols_m[:, lanes], preferred_element_type=jnp.float32)
        two = jnp.dot(hid_t[...], cols_g[:, lanes], preferred_element_type=jnp.float32)
        for t in range(3):
            k = 3 * j + t
            part = slice(t * C, (t + 1) * C)
            g_ref[0, pl.ds(pl.multiple_of(k * C, C), C), :] = one[:, part].T
            g_ref[1, pl.ds(pl.multiple_of((26 - k) * C, C), C), :] = two[:, part]
        return carry

    lax.fori_loop(0, 9, taps_step, 0)


def reduce_kernel(
    sizes, scale, mid_ref, x_ref, y_ref, c_ref, w2_ref, w1_ref, own_ref, g_ref, out_ref, o_ref,
    x_got, y_got, c_got, halo_s, halo_r, padded, edge, shifted, w1f, cols, pair_in, chip_out, chip_in, acc, wire_in, gathered,
    pair_s, pair_r, chip_s, chip_r, wire_s, wire_r, back_s, back_r, out_s, out_r, fwd_s, fwd_r,
):
    drift_size, wire_size = sizes
    chips = drift_size // 2
    chunk = TAPS * C // chips
    piece = acc.shape[0] // wire_size
    d = lax.axis_index("drift")
    w = lax.axis_index("wire")
    core = lax.rem(d, 2)
    chip = d // 2
    partner = place(d + 1 - 2 * core, w)
    chip_peers = []
    wire_peers = []
    for i in range(chips):
        chip_peers.append(lax.rem(chip + 1 + i, chips))
    for i in range(wire_size - 1):
        wire_peers.append(lax.rem(w + 1 + i, wire_size))
    chip_places = [place(2 * peer + core, w) for peer in chip_peers[:-1]]
    wire_places = [place(d, peer) for peer in wire_peers]
    halos = (x_got, y_got, c_got)
    near = halo_peers(sizes)
    greet([partner] + chip_places + wire_places + near)
    halo_copies = halo_start(near, (x_ref, y_ref, c_ref), halos, halo_s, halo_r)

    def convolve(field, weight):
        columns(sizes, field, mid_ref, halos, padded, edge, shifted, cols)

        def rows_step(i, carry):
            rows = pl.ds(pl.multiple_of(i * 256, 256), 256)
            value = jnp.dot(cols[rows, :], weight[...], preferred_element_type=jnp.float32)
            out_ref[field, rows, :] = (own_ref[field, rows, :].astype(jnp.float32) + value).astype(
                jnp.bfloat16
            )
            return carry

        lax.fori_loop(0, ROWS // 256, rows_step, 0)

    def send(src, dst, send_sem, recv_sem, peer):
        copy = pltpu.make_async_remote_copy(
            src_ref=src, dst_ref=dst, send_sem=send_sem, recv_sem=recv_sem,
            device_id=peer, device_id_type=MESH,
        )
        copy.start()
        return copy

    def span(index, size):
        return pl.ds(pl.multiple_of(index * size, 16), size)

    pair = []
    for i, peer in enumerate(chip_peers):
        pair.append(
            send(
                g_ref.at[1 - core, span(peer, chunk)], pair_in.at[i],
                pair_s.at[i], pair_r.at[i], partner,
            )
        )
    acc[...] = jnp.zeros_like(acc)
    flip(w1_ref, w1f)
    ring = []
    for i, peer in enumerate(chip_peers):
        pair[i].wait_recv()
        total = g_ref[core, span(peer, chunk), :] + pair_in[i]
        if i < chips - 1:
            chip_out[i] = total.astype(jnp.bfloat16)
            ring.append(
                send(chip_out.at[i], chip_in.at[i], chip_s.at[i], chip_r.at[i], chip_places[i])
            )
        else:
            acc[0:chunk, :] = total
    for copy in halo_copies:
        copy.wait()
    convolve(0, w2_ref)
    for i, copy in enumerate(ring):
        copy.wait_recv()
        acc[0:chunk, :] += chip_in[i].astype(jnp.float32)
    wires = []
    for i, peer in enumerate(wire_peers):
        wires.append(
            send(
                acc.at[span(peer, piece)], wire_in.at[i], wire_s.at[i], wire_r.at[i],
                wire_places[i],
            )
        )
    convolve(1, w1f)
    own = acc[span(w, piece), :]
    for i, copy in enumerate(wires):
        copy.wait_recv()
        own = own + wire_in[i]
    gathered[span(w, piece), :] = (own * scale).astype(jnp.bfloat16)
    back = []
    for i in range(wire_size - 1):
        mine = gathered.at[span(w, piece)]
        back.append(send(mine, mine, back_s.at[i], back_r.at[i], wire_places[i]))
    for copy in back:
        copy.wait_recv()
    full = gathered.at[0:chunk]
    spot = o_ref.at[core, span(chip, chunk)]
    outs = []
    for i in range(chips - 1):
        outs.append(send(full, spot, out_s.at[i], out_r.at[i], chip_places[i]))
    forwards = [send(full, spot, fwd_s.at[chips - 1], fwd_r.at[chips - 1], partner)]
    o_ref[core, span(chip, chunk), :] = gathered[0:chunk, :]
    for i in range(chips - 1):
        outs[i].wait_recv()
        source = lax.rem(chip + 2 * chips - 1 - i, chips)
        part = o_ref.at[core, span(source, chunk)]
        forwards.append(send(part, part, fwd_s.at[i], fwd_r.at[i], partner))
    for copy in forwards:
        copy.wait_recv()
    for copy in pair + ring + wires + back + outs + forwards:
        copy.wait_send()


def work_scratch():
    return [
        pltpu.VMEM((1360, C), jnp.float32),
        pltpu.VMEM((112, C), jnp.float32),
        pltpu.VMEM((14, 96, C), jnp.bfloat16),
        pltpu.VMEM((TAPS * C, C), jnp.bfloat16),
        pltpu.VMEM((ROWS, TAPS * C), jnp.bfloat16),
    ]


def first_stage(sizes, dense, first_weight, second_weight, mask):
    vmem = pl.BlockSpec(memory_space=pltpu.VMEM)
    return pl.pallas_call(
        functools.partial(first_kernel, sizes),
        out_shape=[
            jax.ShapeDtypeStruct((2, ROWS, C), jnp.bfloat16),
            jax.ShapeDtypeStruct((2, TAPS * C, C), jnp.float32),
        ],
        in_specs=[vmem] * 7,
        out_specs=[vmem] * 2,
        scratch_shapes=halo_scratch()
        + work_scratch()
        + [
            pltpu.VMEM((ROWS, TAPS * C), jnp.bfloat16),
            pltpu.VMEM((C, ROWS), jnp.bfloat16),
            pltpu.VMEM((C, ROWS), jnp.bfloat16),
        ],
        compiler_params=pltpu.CompilerParams(
            collective_id=0, has_side_effects=True, vmem_limit_bytes=48 << 20
        ),
        name="first",
    )(dense.reshape(2, ROWS, C), *faces(dense), first_weight, second_weight, mask)


def second_stage(sizes, scale, middle, first_weight, second_weight, dense, grads):
    drift_size, wire_size = sizes
    chips = drift_size // 2
    chunk = TAPS * C // chips
    piece = -(-chunk // (wire_size * 16)) * 16
    vmem = pl.BlockSpec(memory_space=pltpu.VMEM)
    dma = pltpu.SemaphoreType.DMA
    return pl.pallas_call(
        functools.partial(reduce_kernel, sizes, scale),
        out_shape=[
            jax.ShapeDtypeStruct((2, ROWS, C), jnp.bfloat16),
            jax.ShapeDtypeStruct((2, TAPS * C, C), jnp.bfloat16),
        ],
        in_specs=[vmem] * 8,
        out_specs=[vmem] * 2,
        scratch_shapes=halo_scratch()
        + work_scratch()
        + [
            pltpu.VMEM((chips, chunk, C), jnp.float32),
            pltpu.VMEM((chips - 1, chunk, C), jnp.bfloat16),
            pltpu.VMEM((chips - 1, chunk, C), jnp.bfloat16),
            pltpu.VMEM((piece * wire_size, C), jnp.float32),
            pltpu.VMEM((wire_size - 1, piece, C), jnp.float32),
            pltpu.VMEM((piece * wire_size, C), jnp.bfloat16),
            dma((chips,)), dma((chips,)),
            dma((chips - 1,)), dma((chips - 1,)),
            dma((wire_size - 1,)), dma((wire_size - 1,)),
            dma((wire_size - 1,)), dma((wire_size - 1,)),
            dma((chips - 1,)), dma((chips - 1,)),
            dma((chips,)), dma((chips,)),
        ],
        compiler_params=pltpu.CompilerParams(
            collective_id=1, has_side_effects=True, vmem_limit_bytes=48 << 20
        ),
        name="second",
    )(
        middle, *faces(middle.reshape(2, 12, 4, 16, C)), second_weight, first_weight,
        dense.reshape(2, ROWS, C), grads,
    )


def on_device(features, first_weight, second_weight, cotangent, counts, kernel_map, send_lists):
    sizes = (lax.axis_size("drift"), lax.axis_size("wire"))
    lists = send_lists[0, 0]
    count = counts[0, 0]
    spread = jnp.sum(jnp.where(LISTED, lists[None, :], 0), axis=1)
    active_around = (spread < 9) & AROUND
    centre = jnp.where(
        count > jnp.sum(active_around.astype(jnp.int32)),
        jnp.sum((active_around & BEFORE).astype(jnp.int32)),
        9,
    )
    slots = jnp.where(AROUND, spread, centre)
    live_pos = slots < 9

    both = jnp.stack([features[0, 0], cotangent[0, 0]]).reshape(2, 9, 64, C)
    picked = jnp.take(both, jnp.minimum(slots, 8), axis=1)
    picked = jnp.where(live_pos[None, :, None, None], picked, jnp.zeros_like(picked))
    dense = picked.reshape(2, 3, 3, 4, 4, 4, C).transpose(0, 1, 3, 5, 2, 4, 6)
    dense = jnp.pad(dense.reshape(2, 12, 4, 12, C), ((0, 0), (0, 0), (0, 0), (1, 3), (0, 0)))

    mask = jnp.broadcast_to(live_pos.reshape(3, 1, 1, 3, 1, 1), (3, 4, 4, 3, 4, C))
    mask = jnp.pad(
        mask.astype(jnp.float32).reshape(12, 4, 12, C), ((0, 0), (0, 0), (1, 3), (0, 0))
    ).reshape(ROWS, C)

    first_rows = first_weight.reshape(TAPS * C, C)
    second_rows = second_weight.reshape(TAPS * C, C)
    middle, grads = first_stage(sizes, dense, first_rows, second_rows, mask)
    scale = 1.0 / math.sqrt(float(sizes[0] * sizes[1] * 576))
    summed, reduced = second_stage(
        sizes, scale, middle, first_rows, second_rows, dense, grads
    )

    blocks = summed.reshape(2, 3, 4, 4, 16, C)[:, :, :, :, 1:13]
    blocks = blocks.reshape(2, 3, 4, 4, 3, 4, C).transpose(0, 1, 4, 2, 5, 3, 6)
    blocks = blocks.reshape(2, 9, 64, C)
    slot_ids = jnp.arange(9, dtype=jnp.int32)
    matches = slots[None, :] == slot_ids[:, None]
    positions = jnp.sum(jnp.where(matches, slot_ids[None, :], 0), axis=1)
    placed = jnp.take(blocks, positions, axis=1)
    placed = jnp.where((slot_ids < count)[None, :, None, None], placed, jnp.zeros_like(placed))
    placed = placed.reshape(2, 1, 1, 576, C)
    weights = reduced.astype(jnp.float32).reshape(2, TAPS, C, C)
    return placed[0], placed[1], weights[0], weights[1]


def solution(mesh):
    placed = (
        P("drift", "wire", None, None),
        P(),
        P(),
        P("drift", "wire", None, None),
        P("drift", "wire"),
        P("drift", "wire", None, None),
        P("drift", "wire", None),
    )
    return jax.shard_map(
        on_device,
        mesh=mesh,
        in_specs=placed,
        out_specs=(P("drift", "wire", None, None), P("drift", "wire", None, None), P(), P()),
        check_vma=False,
    )
```

time: 138 us -> 91.3 us (0.66)
  local copies, waits for them, and re-layouts: 27.1 us -> 6.11 us
  Pallas kernels: 94.8 us -> 77.8 us
  other arithmetic: 12.2 us -> 4.22 us
    pallas_call x5 -> x2, Pallas kernels: 94.8 us -> 77.8 us  [the longest x1 52.5 us: second_stage(): pl.pallas_call(functools.partial(reduce_kernel, sizes, scale), out_shape=...]
    transpose x4 -> x0, local copies, waits for them, and re-layouts: 5.78 us -> none  [flipped(): return jnp.transpose(weight[::-1], (0, 2, 1)).reshape(TAPS * C, C)]
    select_n x8 -> x0, other arithmetic: 5.59 us -> none  [the longest x6 4.49 us: keep(): return jnp.where(ok, value, jnp.zeros_like(value))]
    concatenate x1 -> x0, local copies, waits for them, and re-layouts: 5.15 us -> none  [on_device(): slots = jnp.concatenate([around[:4], centre[None], around[4:]])]
    another operation x2, local copies, waits for them, and re-layouts: 5.17 us -> 0.03 us  [faces(): x_send = jnp.stack([fields[:, 0], fields[:, 11]])]
    another operation x7 -> x6, other arithmetic: 3.74 us -> 0.05 us  [the longest x2 0.02 us: faces(): jnp.stack([fields[:, x, :, y] for x in (0, 11) for y in (1, 12)])]
    slice x3 -> x4, local copies, waits for them, and re-layouts: 1.65 us -> 0.16 us  [the longest x2 0.13 us: faces(): fields[:, :, :, 1]]
    slice x2, local copies, waits for them, and re-layouts: 4.18 us -> 2.75 us  [on_device(): return (placed[0], placed[1], weights[0], weights[1])]
where the time goes in v2:
time: 91.3 us; the launch traced here: 91 us
  Pallas kernels  77.8 us (85%)
  local copies, waits for them, and re-layouts  6.11 us (7%)
  other arithmetic  4.22 us (5%)
  between operations  2.89 us (3%)
    pallas_call x1, Pallas kernels, second_stage(): pl.pallas_call(functools.partial(reduce_kernel, sizes, scale), out_shape=...  52.5 us
    pallas_call x1, Pallas kernels, first_stage(): pl.pallas_call(functools.partial(first_kernel, sizes), out_shape=[jax.Sha...  25.4 us
    slice x2, local copies, waits for them, and re-layouts, on_device(): return (placed[0], placed[1], weights[0], weights[1])  2.75 us

profile of v2, /device:TPU:1, one launch (start us, length us, event | category | flops | bytes accessed | tf_op | source)
XLA Modules:
  0.0 91.0 jit_solution(7159392171164779053)
XLA Ops:
  0.6 0.8 select_reduce_fusion.1
  1.4 1.3 %fusion = (s32[]{:T(128)}, s32[]{:T(128)}) fusion(pred[9]{0:T(512)(128)(4,1)} %constant.30.clone, pred[9]{0:T(512)(128)(4,1)} %constant.29.clone, s32[9]{0:T(128)S(1)} %select_reduce_fusion.1), kind=kLoop, calls=%fused_computation.26 | loop fusion | flops 61 | bytes 62 | tf_op jit(solution)/shard_map/reduce_sum | solution.py:368
  4.7 0.7 fusion.1
  5.4 1.0 %pad_maximum_fusion = bf16[2,9,64,128]{3,2,1,0:T(8,128)(2,1)S(1)} fusion(bf16[1,9,64,128]{3,2,1,0:T(8,128)(2,1)} %bitcast.71, bf16[1,9,64,128]{3,2,1,0:T(8,128)(2,1)} %bitcast.72), kind=kLoop, calls=%fused_computation.2 | loop fusion | flops 147456 | bytes 589824 | tf_op jit(solution)/shard_map/stack | solution.py:374
  6.4 0.6 gather_fusion
  7.0 0.1 bitcast_select_fusion.1
  7.2 0.1 copy.35
  7.3 0.1 copy.36
  7.4 0.0 copy-start
  7.4 0.0 copy-start.1
  7.6 0.1 pad.8.clone
  7.7 0.1 reshape.110
  7.8 0.1 broadcast_in_dim.72
  7.9 0.1 broadcast_in_dim.73
  8.0 0.1 broadcast_in_dim.74
  8.1 0.5 copy-done
  8.6 0.3 copy-done.1
  8.8 25.4 %first.1 = (bf16[2,768,128]{2,1,0:T(8,128)(2,1)S(1)}, f32[2,3456,128]{2,1,0:T(8,128)}) custom-call(bf16[2,768,128]{2,1,0:T(8,128)(2,1)S(1)} %bitcast.56, bf16[2,2,4,16,128]{4,3,2,1,0:T(8,128)(2,1)S(1)} %pad_maximum_fusion.1.x_ref, bf16[2,96,128]{2,1,0:T(8,128)(2,1)S(1)} %pad_maximum_fusion.3.y_ref, bf16[4,8,128]{2,1,0:T(8,128)(2,1)S(1)} %pad_maximum_fusion.5.c_ref, ...), custom_call_target="tpu_custom_call" | custom-call | tf_op jit(solution)/shard_map/first/pallas_call | solution.py:297
  34.3 0.1 fusion.4
  34.5 52.5 %second.1 = (bf16[2,768,128]{2,1,0:T(8,128)(2,1)S(1)}, bf16[2,3456,128]{2,1,0:T(8,128)(2,1)S(1)}) custom-call(bf16[2,768,128]{2,1,0:T(8,128)(2,1)S(1)} %get-tuple-element.9.mid_ref, bf16[2,2,4,16,128]{4,3,2,1,0:T(8,128)(2,1)S(1)} %pad_maximum_fusion.2.x_ref, bf16[2,96,128]{2,1,0:T(8,128)(2,1)S(1)} %pad_maximum_fusion.4.y_ref, ...), custom_call_target="tpu_custom_call" | custom-call | tf_op jit(solution)/shard_map/second/pallas_call | solution.py:326
  87.0 2.0 %fusion.2 = (f32[1,3456,128]{2,1,0:T(8,128)}, f32[1,3456,128]{2,1,0:T(8,128)}) fusion(bf16[2,3456,128]{2,1,0:T(8,128)(2,1)S(1)} %get-tuple-element.12), kind=kLoop, calls=%fused_computation.32 | loop fusion | bytes 7077888 | tf_op jit(solution)/shard_map/slice | solution.py:403
  89.0 0.1 slice.112
  89.1 0.1 copy.50
  89.3 0.1 copy.41
  89.4 0.1 select_reduce_fusion
  89.6 0.6 gather_fusion.1
  90.2 0.1 bitcast_select_fusion
  90.3 0.7 fusion.5
  (25 shorter events, 0.3 us)
Async XLA Ops:
  7.4 1.2 %copy-start = (bf16[27,128,128]{2,1,0:T(8,128)(2,1)S(1)}, bf16[27,128,128]{2,1,0:T(8,128)(2,1)}, u32[]{:S(2)}) copy-start(bf16[27,128,128]{2,1,0:T(8,128)(2,1)} %param.13) | copy-start | bytes 2654212
  7.4 1.4 %copy-start.1 = (bf16[27,128,128]{2,1,0:T(8,128)(2,1)S(1)}, bf16[27,128,128]{2,1,0:T(8,128)(2,1)}, u32[]{:S(2)}) copy-start(bf16[27,128,128]{2,1,0:T(8,128)(2,1)} %param.14) | copy-start | bytes 2654212

commit v3 on v2

v3 whole, which is shorter than its diff:
```python
import functools
import math

import jax
import jax.numpy as jnp
import numpy as np
from jax import lax
from jax.experimental import pallas as pl
from jax.experimental.pallas import tpu as pltpu
from jax.sharding import PartitionSpec as P

C = 128
PLANES = 12 * 4
ROWS = PLANES * 16
TAPS = 27
LISTED = np.arange(16)[None, :] == np.array([0, 1, 2, 7, -1, 10, 3, 4, 5])[:, None]
AROUND = np.arange(9) != 4
BEFORE = np.arange(9) < 4
MESH = pl.DeviceIdType.MESH
NEIGHBOURS = ((-1, 0), (1, 0), (0, -1), (0, 1), (-1, -1), (-1, 1), (1, -1), (1, 1))


def place(drift, wire):
    return (drift, wire)


def greet(peers):
    barrier = pltpu.get_barrier_semaphore()
    for peer in peers:
        pl.semaphore_signal(barrier, inc=1, device_id=peer, device_id_type=MESH)
    pl.semaphore_wait(barrier, len(peers))


def halo_peers(sizes):
    d = lax.axis_index("drift")
    w = lax.axis_index("wire")
    return [
        place(lax.rem(d + dd + sizes[0], sizes[0]), lax.rem(w + ww + sizes[1], sizes[1]))
        for dd, ww in NEIGHBOURS
    ]


def halo_start(peers, sends, halos, send_sem, recv_sem):
    copies = []
    for n, peer in enumerate(peers):
        which, slot = (0, n) if n < 2 else (1, n - 2) if n < 4 else (2, n - 4)
        copy = pltpu.make_async_remote_copy(
            src_ref=sends[which][slot],
            dst_ref=halos[which].at[slot],
            send_sem=send_sem.at[n],
            recv_sem=recv_sem.at[n],
            device_id=peer,
            device_id_type=MESH,
        )
        copy.start()
        copies.append(copy)
    return copies


def halo_scratch():
    return [
        pltpu.VMEM((2, 2, 64, C), jnp.bfloat16),
        pltpu.VMEM((2, 2 * PLANES, C), jnp.bfloat16),
        pltpu.VMEM((4, 8, C), jnp.bfloat16),
        pltpu.SemaphoreType.DMA((8,)),
        pltpu.SemaphoreType.DMA((8,)),
    ]


def faces(fields):
    x_send = jnp.stack([fields[:, 0], fields[:, 11]]).reshape(2, 2, 64, C)
    y_send = jnp.stack([fields[:, :, :, 1], fields[:, :, :, 12]]).reshape(2, 2 * PLANES, C)
    c_send = jnp.stack(
        [fields[:, x, :, y] for x in (0, 11) for y in (1, 12)]
    ).reshape(4, 8, C)
    return x_send, y_send, c_send


def flip(weight, out):
    for k in range(TAPS):
        tap = weight[(26 - k) * C : (27 - k) * C, :].astype(jnp.float32)
        out[k * C : (k + 1) * C, :] = tap.T.astype(jnp.bfloat16)


def columns(sizes, field, own, halos, padded, edge, shifted, out):
    x_got, y_got, c_got = halos
    d = lax.axis_index("drift")
    w = lax.axis_index("wire")
    d_ok = (d > 0, d < sizes[0] - 1)
    w_ok = (w > 0, w < sizes[1] - 1)

    def keep(value, ok):
        value = value.astype(jnp.float32)
        return jnp.where(ok, value, jnp.zeros_like(value))

    padded[...] = jnp.zeros_like(padded)
    for x in range(14):
        start = 8 + (x * 6 + 1) * 16
        if x == 0:
            value = keep(x_got[1, field], d_ok[0])
        elif x == 13:
            value = keep(x_got[0, field], d_ok[1])
        else:
            value = own[field, (x - 1) * 64 : x * 64, :].astype(jnp.float32)
        padded[start : start + 64, :] = value
    for side in range(2):
        edge[0:96, :] = keep(y_got[1 - side], w_ok[side])
        edge[96:104, :] = keep(c_got[3 - side], d_ok[0] & w_ok[side])
        edge[104:112, :] = keep(c_got[1 - side], d_ok[1] & w_ok[side])
        for x in range(14):
            first = 96 if x == 0 else 104 if x == 13 else field * PLANES + (x - 1) * 4
            first = first + (field * 4 if x in (0, 13) else 0)
            start = 8 + (x * 6 + 1) * 16 + 13 * side
            padded[pl.ds(start, 4, stride=16), :] = edge[first : first + 4, :]
    for oy in range(3):
        shifted[...] = padded[7 + oy : 7 + oy + 1344, :].astype(jnp.bfloat16).reshape(14, 96, C)
        for ox in range(3):
            for oz in range(3):
                k = 9 * ox + 3 * oy + oz
                out[:, k * C : (k + 1) * C] = shifted[
                    ox : ox + 12, oz * 16 : oz * 16 + 64, :
                ].reshape(ROWS, C)


def kernel(
    sizes, scale, own_ref, x_ref, y_ref, c_ref, w1_ref, w2_ref, mask_ref, out_ref, o_ref,
    x_got, y_got, c_got, halo_s, halo_r, x_got2, y_got2, c_got2, halo_s2, halo_r2,
    padded, edge, shifted, w1f, cols_m, w2f, cols_g, hid_t, bp_t, mid, wide, y_out, corner, c_out,
    grads, pair_in, chip_out, chip_in, acc, wire_in, gathered,
    pair_s, pair_r, chip_s, chip_r, wire_s, wire_r, back_s, back_r, out_s, out_r, fwd_s, fwd_r,
):
    drift_size, wire_size = sizes
    chips = drift_size // 2
    chunk = TAPS * C // chips
    halves = halves_of(chunk)
    piece = wire_in.shape[2]
    d = lax.axis_index("drift")
    w = lax.axis_index("wire")
    core = lax.rem(d, 2)
    chip = d // 2
    partner = place(d + 1 - 2 * core, w)
    chip_peers = [lax.rem(chip + 1 + i, chips) for i in range(chips)]
    wire_peers = [lax.rem(w + 1 + i, wire_size) for i in range(wire_size - 1)]
    chip_places = [place(2 * peer + core, w) for peer in chip_peers[:-1]]
    wire_places = [place(d, peer) for peer in wire_peers]
    near = halo_peers(sizes)
    greet([partner] + chip_places + wire_places + near)

    def send(src, dst, send_sem, recv_sem, peer):
        copy = pltpu.make_async_remote_copy(
            src_ref=src, dst_ref=dst, send_sem=send_sem, recv_sem=recv_sem,
            device_id=peer, device_id_type=MESH,
        )
        copy.start()
        return copy

    def rows_at(start, size):
        return pl.ds(pl.multiple_of(start, 16), size)

    halos = (x_got, y_got, c_got)
    first_halo = halo_start(
        near,
        ([x_ref.at[n] for n in range(2)], [y_ref.at[n] for n in range(2)],
         [c_ref.at[n] for n in range(4)]),
        halos, halo_s, halo_r,
    )
    flip(w2_ref, w2f)
    flip(w1_ref, w1f)
    acc[...] = jnp.zeros_like(acc)
    for copy in first_halo:
        copy.wait()
    columns(sizes, 0, own_ref, halos, padded, edge, shifted, cols_m)
    columns(sizes, 1, own_ref, halos, padded, edge, shifted, cols_g)

    def rows_step(i, carry):
        rows = pl.ds(pl.multiple_of(i * 256, 256), 256)
        pre = jnp.dot(cols_m[rows, :], w1_ref[...], preferred_element_type=jnp.float32)
        back = jnp.dot(cols_g[rows, :], w2f[...], preferred_element_type=jnp.float32)
        live = mask_ref[rows, :] > 0
        gate = 1.0 / (1.0 + jnp.exp(-pre))
        hid = jnp.where(live, pre / (1.0 + jnp.exp(-pre)), 0.0)
        bp = jnp.where(live, back * (gate * (1.0 + pre * (1.0 - gate))), 0.0)
        mid[0, rows, :] = hid.astype(jnp.bfloat16)
        mid[1, rows, :] = bp.astype(jnp.bfloat16)
        wide[0, rows, :] = hid
        wide[1, rows, :] = bp
        hid_t[:, rows] = hid.T.astype(jnp.bfloat16)
        bp_t[:, rows] = bp.T.astype(jnp.bfloat16)
        return carry

    lax.fori_loop(0, ROWS // 256, rows_step, 0)

    for side in range(2):
        for field in range(2):
            face = wide[field, pl.ds(1 + 11 * side, PLANES, stride=16), :]
            y_out[side, field * PLANES : (field + 1) * PLANES, :] = face.astype(jnp.bfloat16)
            corner[side, field * 4 : field * 4 + 4, :] = wide[
                field, pl.ds(1 + 11 * side, 4, stride=16), :
            ]
            corner[2 + side, field * 4 : field * 4 + 4, :] = wide[
                field, pl.ds(704 + 1 + 11 * side, 4, stride=16), :
            ]
    c_out[...] = corner[...].astype(jnp.bfloat16)
    halos2 = (x_got2, y_got2, c_got2)
    second_halo = halo_start(
        near,
        ([mid.at[:, 0:64], mid.at[:, 704:768]], [y_out.at[n] for n in range(2)],
         [c_out.at[n] for n in range(4)]),
        halos2, halo_s2, halo_r2,
    )

    def taps_step(j, carry):
        lanes = pl.ds(pl.multiple_of(j * 3 * C, C), 3 * C)
        one = jnp.dot(bp_t[...], cols_m[:, lanes], preferred_element_type=jnp.float32)
        two = jnp.dot(hid_t[...], cols_g[:, lanes], preferred_element_type=jnp.float32)
        for t in range(3):
            k = 3 * j + t
            part = slice(t * C, (t + 1) * C)
            grads[0, pl.ds(pl.multiple_of(k * C, C), C), :] = one[:, part].T
            grads[1, pl.ds(pl.multiple_of((26 - k) * C, C), C), :] = two[:, part]
        return carry

    pair = []
    for third in range(3):
        lax.fori_loop(3 * third, 3 * third + 3, taps_step, 0)
        part = rows_at(9 * C * (core * third + (1 - core) * (2 - third)), 9 * C)
        pair.append(
            send(
                grads.at[1 - core, part], pair_in.at[part],
                pair_s.at[third], pair_r.at[third], partner,
            )
        )

    for copy in second_halo:
        copy.wait()
    columns(sizes, 0, mid, halos2, padded, edge, shifted, cols_m)
    for copy in pair:
        copy.wait_recv()

    def convolve(field, weight, cols):
        def step(i, carry):
            rows = pl.ds(pl.multiple_of(i * 256, 256), 256)
            value = jnp.dot(cols[rows, :], weight[...], preferred_element_type=jnp.float32)
            out_ref[field, rows, :] = (own_ref[field, rows, :].astype(jnp.float32) + value).astype(
                jnp.bfloat16
            )
            return carry

        lax.fori_loop(0, ROWS // 256, step, 0)

    ring = ([], [])
    for h, (start, size) in enumerate(halves):
        for i, peer in enumerate(chip_peers):
            rows = rows_at(peer * chunk + start, size)
            total = grads[core, rows, :] + pair_in[rows, :]
            if i < chips - 1:
                chip_out[i, start : start + size, :] = total.astype(jnp.bfloat16)
                part = (i, slice(start, start + size))
                ring[h].append(
                    send(
                        chip_out.at[part], chip_in.at[part],
                        chip_s.at[h, i], chip_r.at[h, i], chip_places[i],
                    )
                )
            else:
                acc[h, 0:size, :] = total

    def to_wire(h):
        size = halves[h][1]
        for i, copy in enumerate(ring[h]):
            copy.wait_recv()
            start = halves[h][0]
            acc[h, 0:size, :] += chip_in[i, start : start + size, :].astype(jnp.float32)
        return [
            send(
                acc.at[h, rows_at(peer * piece, piece)], wire_in.at[h, i],
                wire_s.at[h, i], wire_r.at[h, i], wire_places[i],
            )
            for i, peer in enumerate(wire_peers)
        ]

    def from_wire(h, wires):
        own = acc[h, rows_at(w * piece, piece), :]
        for i, copy in enumerate(wires):
            copy.wait_recv()
            own = own + wire_in[h, i]
        mine = rows_at(w * piece, piece)
        gathered[h, mine, :] = (own * scale).astype(jnp.bfloat16)
        return [
            send(
                gathered.at[h, mine], gathered.at[h, mine],
                back_s.at[h, i], back_r.at[h, i], wire_places[i],
            )
            for i in range(wire_size - 1)
        ]

    def to_chips(h, back):
        for copy in back:
            copy.wait_recv()
        start, size = halves[h]
        full = gathered.at[h, 0:size]
        rows = rows_at(chip * chunk + start, size)
        spot = o_ref.at[core, rows]
        sent = [
            send(full, spot, out_s.at[h, i], out_r.at[h, i], chip_places[i])
            for i in range(chips - 1)
        ]
        ahead = send(full, spot, fwd_s.at[h, chips - 1], fwd_r.at[h, chips - 1], partner)
        o_ref[core, rows, :] = gathered[h, 0:size, :]
        return sent, [ahead]

    convolve(0, w2_ref, cols_m)
    wires0 = to_wire(0)
    columns(sizes, 1, mid, halos2, padded, edge, shifted, cols_g)
    convolve(1, w1f, cols_g)
    wires1 = to_wire(1)
    back0 = from_wire(0, wires0)
    back1 = from_wire(1, wires1)
    outs0, forwards0 = to_chips(0, back0)
    outs1, forwards1 = to_chips(1, back1)
    forwards = forwards0 + forwards1
    for h, outs in enumerate((outs0, outs1)):
        start, size = halves[h]
        for i in range(chips - 1):
            outs[i].wait_recv()
            source = lax.rem(chip + 2 * chips - 1 - i, chips)
            part = o_ref.at[core, rows_at(source * chunk + start, size)]
            forwards.append(send(part, part, fwd_s.at[h, i], fwd_r.at[h, i], partner))
    for copy in forwards:
        copy.wait_recv()
    sent = pair + ring[0] + ring[1] + wires0 + wires1 + back0 + back1 + outs0 + outs1 + forwards
    for copy in sent:
        copy.wait_send()


def halves_of(chunk):
    first = (chunk // 16 + 1) // 2 * 16
    return ((0, first), (first, chunk - first))


def work_scratch():
    return [
        pltpu.VMEM((1360, C), jnp.float32),
        pltpu.VMEM((112, C), jnp.float32),
        pltpu.VMEM((14, 96, C), jnp.bfloat16),
        pltpu.VMEM((TAPS * C, C), jnp.bfloat16),
        pltpu.VMEM((ROWS, TAPS * C), jnp.bfloat16),
    ]


def run(sizes, scale, first_weight, second_weight, dense, mask):
    drift_size, wire_size = sizes
    chips = drift_size // 2
    chunk = TAPS * C // chips
    piece = -(-halves_of(chunk)[0][1] // (wire_size * 16)) * 16
    vmem = pl.BlockSpec(memory_space=pltpu.VMEM)
    dma = pltpu.SemaphoreType.DMA
    return pl.pallas_call(
        functools.partial(kernel, sizes, scale),
        out_shape=[
            jax.ShapeDtypeStruct((2, ROWS, C), jnp.bfloat16),
            jax.ShapeDtypeStruct((2, TAPS * C, C), jnp.bfloat16),
        ],
        in_specs=[vmem] * 7,
        out_specs=[vmem] * 2,
        scratch_shapes=halo_scratch()
        + halo_scratch()
        + work_scratch()
        + [
            pltpu.VMEM((TAPS * C, C), jnp.bfloat16),
            pltpu.VMEM((ROWS, TAPS * C), jnp.bfloat16),
            pltpu.VMEM((C, ROWS), jnp.bfloat16),
            pltpu.VMEM((C, ROWS), jnp.bfloat16),
            pltpu.VMEM((2, ROWS, C), jnp.bfloat16),
            pltpu.VMEM((2, ROWS, C), jnp.float32),
            pltpu.VMEM((2, 2 * PLANES, C), jnp.bfloat16),
            pltpu.VMEM((4, 8, C), jnp.float32),
            pltpu.VMEM((4, 8, C), jnp.bfloat16),
            pltpu.VMEM((2, TAPS * C, C), jnp.float32),
            pltpu.VMEM((TAPS * C, C), jnp.float32),
            pltpu.VMEM((chips - 1, chunk, C), jnp.bfloat16),
            pltpu.VMEM((chips - 1, chunk, C), jnp.bfloat16),
            pltpu.VMEM((2, piece * wire_size, C), jnp.float32),
            pltpu.VMEM((2, wire_size - 1, piece, C), jnp.float32),
            pltpu.VMEM((2, piece * wire_size, C), jnp.bfloat16),
            dma((3,)), dma((3,)),
            dma((2, chips - 1)), dma((2, chips - 1)),
            dma((2, wire_size - 1)), dma((2, wire_size - 1)),
            dma((2, wire_size - 1)), dma((2, wire_size - 1)),
            dma((2, chips - 1)), dma((2, chips - 1)),
            dma((2, chips)), dma((2, chips)),
        ],
        compiler_params=pltpu.CompilerParams(
            collective_id=0, has_side_effects=True, vmem_limit_bytes=52 << 20
        ),
        name="layers",
    )(dense.reshape(2, ROWS, C), *faces(dense), first_weight, second_weight, mask)


def on_device(features, first_weight, second_weight, cotangent, counts, kernel_map, send_lists):
    sizes = (lax.axis_size("drift"), lax.axis_size("wire"))
    lists = send_lists[0, 0]
    count = counts[0, 0]
    spread = jnp.sum(jnp.where(LISTED, lists[None, :], 0), axis=1)
    active_around = (spread < 9) & AROUND
    centre = jnp.where(
        count > jnp.sum(active_around.astype(jnp.int32)),
        jnp.sum((active_around & BEFORE).astype(jnp.int32)),
        9,
    )
    slots = jnp.where(AROUND, spread, centre)
    live_pos = slots < 9

    both = jnp.stack([features[0, 0], cotangent[0, 0]]).reshape(2, 9, 64, C)
    picked = jnp.take(both, jnp.minimum(slots, 8), axis=1)
    picked = jnp.where(live_pos[None, :, None, None], picked, jnp.zeros_like(picked))
    dense = picked.reshape(2, 3, 3, 4, 4, 4, C).transpose(0, 1, 3, 5, 2, 4, 6)
    dense = jnp.pad(dense.reshape(2, 12, 4, 12, C), ((0, 0), (0, 0), (0, 0), (1, 3), (0, 0)))

    mask = jnp.broadcast_to(live_pos.reshape(3, 1, 1, 3, 1, 1), (3, 4, 4, 3, 4, C))
    mask = jnp.pad(
        mask.astype(jnp.float32).reshape(12, 4, 12, C), ((0, 0), (0, 0), (1, 3), (0, 0))
    ).reshape(ROWS, C)

    first_rows = first_weight.reshape(TAPS * C, C)
    second_rows = second_weight.reshape(TAPS * C, C)
    scale = 1.0 / math.sqrt(float(sizes[0] * sizes[1] * 576))
    summed, reduced = run(sizes, scale, first_rows, second_rows, dense, mask)

    blocks = summed.reshape(2, 3, 4, 4, 16, C)[:, :, :, :, 1:13]
    blocks = blocks.reshape(2, 3, 4, 4, 3, 4, C).transpose(0, 1, 4, 2, 5, 3, 6)
    blocks = blocks.reshape(2, 9, 64, C)
    slot_ids = jnp.arange(9, dtype=jnp.int32)
    matches = slots[None, :] == slot_ids[:, None]
    positions = jnp.sum(jnp.where(matches, slot_ids[None, :], 0), axis=1)
    placed = jnp.take(blocks, positions, axis=1)
    placed = jnp.where((slot_ids < count)[None, :, None, None], placed, jnp.zeros_like(placed))
    placed = placed.reshape(2, 1, 1, 576, C)
    weights = reduced.astype(jnp.float32).reshape(2, TAPS, C, C)
    return placed[0], placed[1], weights[0], weights[1]


def solution(mesh):
    placed = (
        P("drift", "wire", None, None),
        P(),
        P(),
        P("drift", "wire", None, None),
        P("drift", "wire"),
        P("drift", "wire", None, None),
        P("drift", "wire", None),
    )
    return jax.shard_map(
        on_device,
        mesh=mesh,
        in_specs=placed,
        out_specs=(P("drift", "wire", None, None), P("drift", "wire", None, None), P(), P()),
        check_vma=False,
    )
```

time: 91.3 us -> 80.2 us (0.88)
  Pallas kernels: 77.8 us -> 67.8 us
  local copies, waits for them, and re-layouts: 6.11 us -> 5.17 us
    pallas_call x2 -> x1, Pallas kernels: 77.8 us -> 67.8 us  [run(): pl.pallas_call(functools.partial(kernel, sizes, scale), out_shape=[jax.Sh...]
where the time goes in v3:
time: 80.2 us; the launch traced here: 80 us
  Pallas kernels  67.8 us (85%)
  local copies, waits for them, and re-layouts  5.17 us (6%)
  other arithmetic  4.19 us (5%)
  between operations  2.79 us (3%)
    pallas_call x1, Pallas kernels, run(): pl.pallas_call(functools.partial(kernel, sizes, scale), out_shape=[jax.Sh...  67.8 us
    slice x2, local copies, waits for them, and re-layouts, on_device(): return (placed[0], placed[1], weights[0], weights[1])  2.75 us

profile of v3, /device:TPU:1, one launch (start us, length us, event | category | flops | bytes accessed | tf_op | source)
XLA Modules:
  0.0 80.0 jit_solution(10207904005162286676)
XLA Ops:
  1.3 0.8 %select_reduce_fusion.1 = s32[9]{0:T(128)S(1)} fusion(pred[9,16]{1,0:T(8,128)(4,1)} %constant.28.clone, s32[16]{0:T(128)} %bitcast.61), kind=kLoop, calls=%fused_computation.10 | loop fusion | flops 279 | bytes 244 | tf_op jit(solution)/shard_map/reduce_sum | solution.py:404
  2.1 1.3 %fusion = (s32[]{:T(128)}, s32[]{:T(128)}) fusion(pred[9]{0:T(512)(128)(4,1)} %constant.30.clone, pred[9]{0:T(512)(128)(4,1)} %constant.29.clone, s32[9]{0:T(128)S(1)} %select_reduce_fusion.1), kind=kLoop, calls=%fused_computation.19 | loop fusion | flops 61 | bytes 62 | tf_op jit(solution)/shard_map/reduce_sum | solution.py:408
  4.7 0.7 fusion.1
  5.4 0.1 select_reduce_fusion
  5.5 0.1 reshape.96
  5.6 0.1 broadcast_in_dim.72
  5.7 0.1 broadcast_in_dim.73
  5.8 1.0 %pad_maximum_fusion = bf16[2,9,64,128]{3,2,1,0:T(8,128)(2,1)S(1)} fusion(bf16[1,9,64,128]{3,2,1,0:T(8,128)(2,1)} %bitcast.49, bf16[1,9,64,128]{3,2,1,0:T(8,128)(2,1)} %bitcast.50), kind=kLoop, calls=%fused_computation.2 | loop fusion | flops 147456 | bytes 589824 | tf_op jit(solution)/shard_map/stack | solution.py:414
  6.8 0.6 gather_fusion
  7.4 0.1 bitcast_select_fusion.1
  7.5 0.1 copy.27
  7.8 0.1 copy.36
  7.9 0.1 pad.8.clone
  8.1 0.1 broadcast_in_dim.74
  8.2 67.8 %layers.1 = (bf16[2,768,128]{2,1,0:T(8,128)(2,1)S(1)}, bf16[2,3456,128]{2,1,0:T(8,128)(2,1)}) custom-call(bf16[2,768,128]{2,1,0:T(8,128)(2,1)S(1)} %bitcast.35, bf16[2,2,64,128]{3,2,1,0:T(8,128)(2,1)S(1)} %pad_maximum_fusion.1.x_ref, bf16[2,96,128]{2,1,0:T(8,128)(2,1)S(1)} %pad_maximum_fusion.2.y_ref, bf16[4,8,128]{2,1,0:T(8,128)(2,1)S(1)} %pad_maximum_fusion.3.c_ref, ...), custom_call_target="tpu_custom_call" | custom-call | tf_op jit(solution)/shard_map/layers/pallas_call | solution.py:358
  76.1 0.0 copy-start
  76.1 0.1 slice.72
  76.2 0.1 copy.35
  76.4 0.1 copy.34
  76.5 0.6 gather_fusion.1
  77.1 0.1 bitcast_select_fusion
  77.2 0.7 fusion.4
  78.0 0.0 copy-done
  78.0 2.0 %fusion.2 = (f32[1,3456,128]{2,1,0:T(8,128)}, f32[1,3456,128]{2,1,0:T(8,128)}) fusion(bf16[2,3456,128]{2,1,0:T(8,128)(2,1)S(1)} %copy-done), kind=kLoop, calls=%fused_computation.25 | loop fusion | bytes 7077888 | tf_op jit(solution)/shard_map/slice | solution.py:440
  (16 shorter events, 0.2 us)
Async XLA Ops:
  76.1 1.9 %copy-start = (bf16[2,3456,128]{2,1,0:T(8,128)(2,1)S(1)}, bf16[2,3456,128]{2,1,0:T(8,128)(2,1)}, u32[]{:S(2)}) copy-start(bf16[2,3456,128]{2,1,0:T(8,128)(2,1)} %get-tuple-element.8) | copy-start | bytes 5308420

commit v4 on v3

--- a/solution.py
+++ b/solution.py
@@ -17,6 +17,7 @@
 AROUND = np.arange(9) != 4
 BEFORE = np.arange(9) < 4
 MESH = pl.DeviceIdType.MESH
+RELATIVE = ((0, 2), (1, 2), (0, 1), (0, 3), (1, 1), (1, 3), (1, 0), (0, 0))
 NEIGHBOURS = ((-1, 0), (1, 0), (0, -1), (0, 1), (-1, -1), (-1, 1), (1, -1), (1, 1))
 
 
@@ -126,8 +127,8 @@
     sizes, scale, own_ref, x_ref, y_ref, c_ref, w1_ref, w2_ref, mask_ref, out_ref, o_ref,
     x_got, y_got, c_got, halo_s, halo_r, x_got2, y_got2, c_got2, halo_s2, halo_r2,
     padded, edge, shifted, w1f, cols_m, w2f, cols_g, hid_t, bp_t, mid, wide, y_out, corner, c_out,
-    grads, pair_in, chip_out, chip_in, acc, wire_in, gathered,
-    pair_s, pair_r, chip_s, chip_r, wire_s, wire_r, back_s, back_r, out_s, out_r, fwd_s, fwd_r,
+    grads, pair_in, chip_out, chip_in, relay_in, acc, wire_in, gathered,
+    pair_s, pair_r, chip_s, chip_r, relay_s, relay_r, wire_s, wire_r, back_s, back_r, out_s, out_r, fwd_s, fwd_r,
 ):
     drift_size, wire_size = sizes
     chips = drift_size // 2
@@ -139,7 +140,16 @@
     core = lax.rem(d, 2)
     chip = d // 2
     partner = place(d + 1 - 2 * core, w)
-    chip_peers = [lax.rem(chip + 1 + i, chips) for i in range(chips)]
+    chip_x, chip_y = chip // 4, lax.rem(chip, 4)
+
+    def chip_at(dx, dy):
+        column = 1 - chip_x if dx else chip_x
+        return column * 4 + lax.rem(chip_y + dy, 4)
+
+    def place_at(dx, dy):
+        return place(2 * chip_at(dx, dy) + core, w)
+
+    chip_peers = [chip_at(dx, dy) for dx, dy in RELATIVE]
     wire_peers = [lax.rem(w + 1 + i, wire_size) for i in range(wire_size - 1)]
     chip_places = [place(2 * peer + core, w) for peer in chip_peers[:-1]]
     wire_places = [place(d, peer) for peer in wire_peers]
@@ -249,6 +259,7 @@
         lax.fori_loop(0, ROWS // 256, step, 0)
 
     ring = ([], [])
+    hops = ([], [])
     for h, (start, size) in enumerate(halves):
         for i, peer in enumerate(chip_peers):
             rows = rows_at(peer * chunk + start, size)
@@ -256,20 +267,40 @@
             if i < chips - 1:
                 chip_out[i, start : start + size, :] = total.astype(jnp.bfloat16)
                 part = (i, slice(start, start + size))
-                ring[h].append(
-                    send(
-                        chip_out.at[part], chip_in.at[part],
-                        chip_s.at[h, i], chip_r.at[h, i], chip_places[i],
+                if i < 2:
+                    hops[h].append(
+                        send(
+                            chip_out.at[part], relay_in.at[part],
+                            chip_s.at[h, i], relay_r.at[h, i], place_at(0, 1 if i == 0 else 3),
+                        )
                     )
-                )
+                else:
+                    ring[h].append(
+                        send(
+                            chip_out.at[part], chip_in.at[part],
+                            chip_s.at[h, i], chip_r.at[h, i], chip_places[i],
+                        )
+                    )
             else:
                 acc[h, 0:size, :] = total
 
+    def relay(h):
+        start, size = halves[h]
+        for i, copy in enumerate(hops[h]):
+            copy.wait_recv()
+            part = (i, slice(start, start + size))
+            ring[h].append(
+                send(
+                    relay_in.at[part], chip_in.at[part], relay_s.at[h, i], chip_r.at[h, i],
+                    place_at(0, 1) if i == 0 else place_at(1, 3),
+                )
+            )
+
     def to_wire(h):
-        size = halves[h][1]
-        for i, copy in enumerate(ring[h]):
+        start, size = halves[h]
+        for n, copy in enumerate(ring[h]):
             copy.wait_recv()
-            start = halves[h][0]
+            i = n + 2 if n < chips - 3 else n - (chips - 3)
             acc[h, 0:size, :] += chip_in[i, start : start + size, :].astype(jnp.float32)
         return [
             send(
@@ -294,41 +325,77 @@
             for i in range(wire_size - 1)
         ]
 
+    forwards = []
+    outs = ({}, {})
+
+    def chip_rows(h, dx, dy):
+        return rows_at(chip_at(dx, dy) * chunk + halves[h][0], halves[h][1])
+
+    def onward(h, n, src, rows):
+        spot = o_ref.at[core, rows]
+        forwards.append(send(src, spot, fwd_s.at[h, n], fwd_r.at[h, n], partner))
+
+    def pass_on(h, kind, src, rows, peer):
+        outs[h][kind] = send(
+            src, o_ref.at[core, rows], out_s.at[h, kind], out_r.at[h, kind], peer
+        )
+
     def to_chips(h, back):
         for copy in back:
             copy.wait_recv()
-        start, size = halves[h]
-        full = gathered.at[h, 0:size]
-        rows = rows_at(chip * chunk + start, size)
-        spot = o_ref.at[core, rows]
-        sent = [
-            send(full, spot, out_s.at[h, i], out_r.at[h, i], chip_places[i])
-            for i in range(chips - 1)
-        ]
-        ahead = send(full, spot, fwd_s.at[h, chips - 1], fwd_r.at[h, chips - 1], partner)
-        o_ref[core, rows, :] = gathered[h, 0:size, :]
-        return sent, [ahead]
+        full = gathered.at[h, 0 : halves[h][1]]
+        rows = chip_rows(h, 0, 0)
+        pass_on(h, 0, full, rows, place_at(1, 0))
+        pass_on(h, 1, full, rows, place_at(0, 1))
+        pass_on(h, 2, full, rows, place_at(0, 3))
+        onward(h, 7, full, rows)
+        o_ref[core, rows, :] = gathered[h, 0 : halves[h][1], :]
+
+    def arrived(h, kind, dx, dy):
+        outs[h][kind].wait_recv()
+        rows = chip_rows(h, dx, dy)
+        part = o_ref.at[core, rows]
+        return part, rows
 
     convolve(0, w2_ref, cols_m)
+    relay(0)
+    columns(sizes, 1, mid, halos2, padded, edge, shifted, cols_g)
+    relay(1)
     wires0 = to_wire(0)
-    columns(sizes, 1, mid, halos2, padded, edge, shifted, cols_g)
     convolve(1, w1f, cols_g)
     wires1 = to_wire(1)
     back0 = from_wire(0, wires0)
     back1 = from_wire(1, wires1)
-    outs0, forwards0 = to_chips(0, back0)
-    outs1, forwards1 = to_chips(1, back1)
-    forwards = forwards0 + forwards1
-    for h, outs in enumerate((outs0, outs1)):
-        start, size = halves[h]
-        for i in range(chips - 1):
-            outs[i].wait_recv()
-            source = lax.rem(chip + 2 * chips - 1 - i, chips)
-            part = o_ref.at[core, rows_at(source * chunk + start, size)]
-            forwards.append(send(part, part, fwd_s.at[h, i], fwd_r.at[h, i], partner))
+    to_chips(0, back0)
+    to_chips(1, back1)
+    for h in range(2):
+        part, rows = arrived(h, 0, 1, 0)
+        pass_on(h, 3, part, rows, place_at(0, 1))
+        pass_on(h, 4, part, rows, place_at(0, 3))
+        onward(h, 0, part, rows)
+        part, rows = arrived(h, 1, 0, 3)
+        if h == 0:
+            pass_on(h, 5, part, rows, place_at(0, 1))
+        onward(h, 1, part, rows)
+        part, rows = arrived(h, 2, 0, 1)
+        if h == 1:
+            pass_on(h, 5, part, rows, place_at(0, 3))
+        onward(h, 2, part, rows)
+    for h in range(2):
+        part, rows = arrived(h, 5, 0, 2)
+        pass_on(h, 6, part, rows, place_at(1, 0))
+        onward(h, 5, part, rows)
+        part, rows = arrived(h, 3, 1, 3)
+        onward(h, 3, part, rows)
+        part, rows = arrived(h, 4, 1, 1)
+        onward(h, 4, part, rows)
+    for h in range(2):
+        part, rows = arrived(h, 6, 1, 2)
+        onward(h, 6, part, rows)
     for copy in forwards:
         copy.wait_recv()
-    sent = pair + ring[0] + ring[1] + wires0 + wires1 + back0 + back1 + outs0 + outs1 + forwards
+    sent = pair + hops[0] + hops[1] + ring[0] + ring[1] + wires0 + wires1 + back0 + back1 + forwards
+    sent = sent + list(outs[0].values()) + list(outs[1].values())
     for copy in sent:
         copy.wait_send()
 
@@ -380,11 +447,13 @@
             pltpu.VMEM((TAPS * C, C), jnp.float32),
             pltpu.VMEM((chips - 1, chunk, C), jnp.bfloat16),
             pltpu.VMEM((chips - 1, chunk, C), jnp.bfloat16),
+            pltpu.VMEM((2, chunk, C), jnp.bfloat16),
             pltpu.VMEM((2, piece * wire_size, C), jnp.float32),
             pltpu.VMEM((2, wire_size - 1, piece, C), jnp.float32),
             pltpu.VMEM((2, piece * wire_size, C), jnp.bfloat16),
             dma((3,)), dma((3,)),
             dma((2, chips - 1)), dma((2, chips - 1)),
+            dma((2, 2)), dma((2, 2)),
             dma((2, wire_size - 1)), dma((2, wire_size - 1)),
             dma((2, wire_size - 1)), dma((2, wire_size - 1)),
             dma((2, chips - 1)), dma((2, chips - 1)),

time: 80.2 us -> 84.4 us (1.052)
  Pallas kernels: 67.8 us -> 72.1 us
    pallas_call x1, Pallas kernels: 67.8 us -> 72.1 us  [run(): pl.pallas_call(functools.partial(kernel, sizes, scale), out_shape=[jax.Sh...]
where the time goes in v4:
time: 84.4 us; the launch traced here: 84.2 us
  Pallas kernels  72.1 us (85%)
  local copies, waits for them, and re-layouts  5.17 us (6%)
  other arithmetic  4.19 us (5%)
  between operations  2.79 us (3%)
    pallas_call x1, Pallas kernels, run(): pl.pallas_call(functools.partial(kernel, sizes, scale), out_shape=[jax.Sh...  72.1 us
    slice x2, local copies, waits for them, and re-layouts, on_device(): return (placed[0], placed[1], weights[0], weights[1])  2.75 us

profile of v4, /device:TPU:1, one launch (start us, length us, event | category | flops | bytes accessed | tf_op | source)
XLA Modules:
  0.0 84.2 jit_solution(5062984438458981262)
XLA Ops:
  1.3 0.8 select_reduce_fusion.1
  2.1 1.3 %fusion = (s32[]{:T(128)}, s32[]{:T(128)}) fusion(pred[9]{0:T(512)(128)(4,1)} %constant.30.clone, pred[9]{0:T(512)(128)(4,1)} %constant.29.clone, s32[9]{0:T(128)S(1)} %select_reduce_fusion.1), kind=kLoop, calls=%fused_computation.19 | loop fusion | flops 61 | bytes 62 | tf_op jit(solution)/shard_map/reduce_sum | solution.py:477
  4.7 0.7 fusion.1
  5.4 0.1 select_reduce_fusion
  5.5 0.1 reshape.96
  5.6 0.1 broadcast_in_dim.72
  5.7 0.1 broadcast_in_dim.73
  5.8 1.0 %pad_maximum_fusion = bf16[2,9,64,128]{3,2,1,0:T(8,128)(2,1)S(1)} fusion(bf16[1,9,64,128]{3,2,1,0:T(8,128)(2,1)} %bitcast.49, bf16[1,9,64,128]{3,2,1,0:T(8,128)(2,1)} %bitcast.50), kind=kLoop, calls=%fused_computation.2 | loop fusion | flops 147456 | bytes 589824 | tf_op jit(solution)/shard_map/stack | solution.py:483
  6.8 0.6 gather_fusion
  7.4 0.1 bitcast_select_fusion.1
  7.5 0.1 copy.27
  7.8 0.1 copy.36
  7.9 0.1 pad.8.clone
  8.1 0.1 broadcast_in_dim.74
  8.2 72.1 %layers.1 = (bf16[2,768,128]{2,1,0:T(8,128)(2,1)S(1)}, bf16[2,3456,128]{2,1,0:T(8,128)(2,1)}) custom-call(bf16[2,768,128]{2,1,0:T(8,128)(2,1)S(1)} %bitcast.35, bf16[2,2,64,128]{3,2,1,0:T(8,128)(2,1)S(1)} %pad_maximum_fusion.1.x_ref, bf16[2,96,128]{2,1,0:T(8,128)(2,1)S(1)} %pad_maximum_fusion.2.y_ref, bf16[4,8,128]{2,1,0:T(8,128)(2,1)S(1)} %pad_maximum_fusion.3.c_ref, ...), custom_call_target="tpu_custom_call" | custom-call | tf_op jit(solution)/shard_map/layers/pallas_call | solution.py:425
  80.3 0.0 copy-start
  80.3 0.1 slice.72
  80.5 0.1 copy.35
  80.6 0.1 copy.34
  80.7 0.6 gather_fusion.1
  81.3 0.1 bitcast_select_fusion
  81.5 0.7 fusion.4
  82.2 0.0 copy-done
  82.2 2.0 %fusion.2 = (f32[1,3456,128]{2,1,0:T(8,128)}, f32[1,3456,128]{2,1,0:T(8,128)}) fusion(bf16[2,3456,128]{2,1,0:T(8,128)(2,1)S(1)} %copy-done), kind=kLoop, calls=%fused_computation.25 | loop fusion | bytes 7077888 | tf_op jit(solution)/shard_map/slice | solution.py:509
  (16 shorter events, 0.2 us)
Async XLA Ops:
  80.3 1.9 %copy-start = (bf16[2,3456,128]{2,1,0:T(8,128)(2,1)S(1)}, bf16[2,3456,128]{2,1,0:T(8,128)(2,1)}, u32[]{:S(2)}) copy-start(bf16[2,3456,128]{2,1,0:T(8,128)(2,1)} %get-tuple-element.8) | copy-start | bytes 5308420

commit v5 on v3

--- a/solution.py
+++ b/solution.py
@@ -313,10 +313,10 @@
     wires0 = to_wire(0)
     columns(sizes, 1, mid, halos2, padded, edge, shifted, cols_g)
     convolve(1, w1f, cols_g)
+    back0 = from_wire(0, wires0)
     wires1 = to_wire(1)
-    back0 = from_wire(0, wires0)
+    outs0, forwards0 = to_chips(0, back0)
     back1 = from_wire(1, wires1)
-    outs0, forwards0 = to_chips(0, back0)
     outs1, forwards1 = to_chips(1, back1)
     forwards = forwards0 + forwards1
     for h, outs in enumerate((outs0, outs1)):

time: 80.2 us -> 80.6 us (level)
  no operation moved by 1% of the time
where the time goes in v5:
time: 80.6 us; the launch traced here: 80.4 us
  Pallas kernels  68.3 us (85%)
  local copies, waits for them, and re-layouts  5.17 us (6%)
  other arithmetic  4.19 us (5%)
  between operations  2.79 us (3%)
    pallas_call x1, Pallas kernels, run(): pl.pallas_call(functools.partial(kernel, sizes, scale), out_shape=[jax.Sh...  68.3 us
    slice x2, local copies, waits for them, and re-layouts, on_device(): return (placed[0], placed[1], weights[0], weights[1])  2.75 us

profile of v5, /device:TPU:1, one launch (start us, length us, event | category | flops | bytes accessed | tf_op | source)
XLA Modules:
  0.0 80.4 jit_solution(9507047982849737115)
XLA Ops:
  1.3 0.8 select_reduce_fusion.1
  2.1 1.3 %fusion = (s32[]{:T(128)}, s32[]{:T(128)}) fusion(pred[9]{0:T(512)(128)(4,1)} %constant.30.clone, pred[9]{0:T(512)(128)(4,1)} %constant.29.clone, s32[9]{0:T(128)S(1)} %select_reduce_fusion.1), kind=kLoop, calls=%fused_computation.19 | loop fusion | flops 61 | bytes 62 | tf_op jit(solution)/shard_map/reduce_sum | solution.py:408
  4.7 0.7 fusion.1
  5.4 0.1 select_reduce_fusion
  5.5 0.1 reshape.96
  5.6 0.1 broadcast_in_dim.72
  5.7 0.1 broadcast_in_dim.73
  5.8 1.0 %pad_maximum_fusion = bf16[2,9,64,128]{3,2,1,0:T(8,128)(2,1)S(1)} fusion(bf16[1,9,64,128]{3,2,1,0:T(8,128)(2,1)} %bitcast.49, bf16[1,9,64,128]{3,2,1,0:T(8,128)(2,1)} %bitcast.50), kind=kLoop, calls=%fused_computation.2 | loop fusion | flops 147456 | bytes 589824 | tf_op jit(solution)/shard_map/stack | solution.py:414
  6.8 0.6 gather_fusion
  7.4 0.1 bitcast_select_fusion.1
  7.5 0.1 copy.27
  7.8 0.1 copy.36
  7.9 0.1 pad.8.clone
  8.1 0.1 broadcast_in_dim.74
  8.2 68.3 %layers.1 = (bf16[2,768,128]{2,1,0:T(8,128)(2,1)S(1)}, bf16[2,3456,128]{2,1,0:T(8,128)(2,1)}) custom-call(bf16[2,768,128]{2,1,0:T(8,128)(2,1)S(1)} %bitcast.35, bf16[2,2,64,128]{3,2,1,0:T(8,128)(2,1)S(1)} %pad_maximum_fusion.1.x_ref, bf16[2,96,128]{2,1,0:T(8,128)(2,1)S(1)} %pad_maximum_fusion.2.y_ref, bf16[4,8,128]{2,1,0:T(8,128)(2,1)S(1)} %pad_maximum_fusion.3.c_ref, ...), custom_call_target="tpu_custom_call" | custom-call | tf_op jit(solution)/shard_map/layers/pallas_call | solution.py:358
  76.5 0.0 copy-start
  76.5 0.1 slice.72
  76.7 0.1 copy.35
  76.8 0.1 copy.34
  77.0 0.6 gather_fusion.1
  77.6 0.1 bitcast_select_fusion
  77.7 0.7 fusion.4
  78.4 0.0 copy-done
  78.4 2.0 %fusion.2 = (f32[1,3456,128]{2,1,0:T(8,128)}, f32[1,3456,128]{2,1,0:T(8,128)}) fusion(bf16[2,3456,128]{2,1,0:T(8,128)(2,1)S(1)} %copy-done), kind=kLoop, calls=%fused_computation.25 | loop fusion | bytes 7077888 | tf_op jit(solution)/shard_map/slice | solution.py:440
  (16 shorter events, 0.2 us)
Async XLA Ops:
  76.5 1.9 %copy-start = (bf16[2,3456,128]{2,1,0:T(8,128)(2,1)S(1)}, bf16[2,3456,128]{2,1,0:T(8,128)(2,1)}, u32[]{:S(2)}) copy-start(bf16[2,3456,128]{2,1,0:T(8,128)(2,1)} %get-tuple-element.8) | copy-start | bytes 5308420

commit v6 on v4

--- a/solution.py
+++ b/solution.py
@@ -127,8 +127,8 @@
     sizes, scale, own_ref, x_ref, y_ref, c_ref, w1_ref, w2_ref, mask_ref, out_ref, o_ref,
     x_got, y_got, c_got, halo_s, halo_r, x_got2, y_got2, c_got2, halo_s2, halo_r2,
     padded, edge, shifted, w1f, cols_m, w2f, cols_g, hid_t, bp_t, mid, wide, y_out, corner, c_out,
-    grads, pair_in, chip_out, chip_in, relay_in, acc, wire_in, gathered,
-    pair_s, pair_r, chip_s, chip_r, relay_s, relay_r, wire_s, wire_r, back_s, back_r, out_s, out_r, fwd_s, fwd_r,
+    grads, pair_in, chip_out, chip_in, acc, wire_in, gathered,
+    pair_s, pair_r, chip_s, chip_r, wire_s, wire_r, back_s, back_r, out_s, out_r, fwd_s, fwd_r,
 ):
     drift_size, wire_size = sizes
     chips = drift_size // 2
@@ -259,7 +259,6 @@
         lax.fori_loop(0, ROWS // 256, step, 0)
 
     ring = ([], [])
-    hops = ([], [])
     for h, (start, size) in enumerate(halves):
         for i, peer in enumerate(chip_peers):
             rows = rows_at(peer * chunk + start, size)
@@ -267,40 +266,20 @@
             if i < chips - 1:
                 chip_out[i, start : start + size, :] = total.astype(jnp.bfloat16)
                 part = (i, slice(start, start + size))
-                if i < 2:
-                    hops[h].append(
-                        send(
-                            chip_out.at[part], relay_in.at[part],
-                            chip_s.at[h, i], relay_r.at[h, i], place_at(0, 1 if i == 0 else 3),
-                        )
+                ring[h].append(
+                    send(
+                        chip_out.at[part], chip_in.at[part],
+                        chip_s.at[h, i], chip_r.at[h, i], chip_places[i],
                     )
-                else:
-                    ring[h].append(
-                        send(
-                            chip_out.at[part], chip_in.at[part],
-                            chip_s.at[h, i], chip_r.at[h, i], chip_places[i],
-                        )
-                    )
+                )
             else:
                 acc[h, 0:size, :] = total
 
-    def relay(h):
-        start, size = halves[h]
-        for i, copy in enumerate(hops[h]):
+    def to_wire(h):
+        size = halves[h][1]
+        for i, copy in enumerate(ring[h]):
             copy.wait_recv()
-            part = (i, slice(start, start + size))
-            ring[h].append(
-                send(
-                    relay_in.at[part], chip_in.at[part], relay_s.at[h, i], chip_r.at[h, i],
-                    place_at(0, 1) if i == 0 else place_at(1, 3),
-                )
-            )
-
-    def to_wire(h):
-        start, size = halves[h]
-        for n, copy in enumerate(ring[h]):
-            copy.wait_recv()
-            i = n + 2 if n < chips - 3 else n - (chips - 3)
+            start = halves[h][0]
             acc[h, 0:size, :] += chip_in[i, start : start + size, :].astype(jnp.float32)
         return [
             send(
@@ -358,10 +337,8 @@
         return part, rows
 
     convolve(0, w2_ref, cols_m)
-    relay(0)
+    wires0 = to_wire(0)
     columns(sizes, 1, mid, halos2, padded, edge, shifted, cols_g)
-    relay(1)
-    wires0 = to_wire(0)
     convolve(1, w1f, cols_g)
     wires1 = to_wire(1)
     back0 = from_wire(0, wires0)
@@ -394,7 +371,7 @@
         onward(h, 6, part, rows)
     for copy in forwards:
         copy.wait_recv()
-    sent = pair + hops[0] + hops[1] + ring[0] + ring[1] + wires0 + wires1 + back0 + back1 + forwards
+    sent = pair + ring[0] + ring[1] + wires0 + wires1 + back0 + back1 + forwards
     sent = sent + list(outs[0].values()) + list(outs[1].values())
     for copy in sent:
         copy.wait_send()
@@ -447,13 +424,11 @@
             pltpu.VMEM((TAPS * C, C), jnp.float32),
             pltpu.VMEM((chips - 1, chunk, C), jnp.bfloat16),
             pltpu.VMEM((chips - 1, chunk, C), jnp.bfloat16),
-            pltpu.VMEM((2, chunk, C), jnp.bfloat16),
             pltpu.VMEM((2, piece * wire_size, C), jnp.float32),
             pltpu.VMEM((2, wire_size - 1, piece, C), jnp.float32),
             pltpu.VMEM((2, piece * wire_size, C), jnp.bfloat16),
             dma((3,)), dma((3,)),
             dma((2, chips - 1)), dma((2, chips - 1)),
-            dma((2, 2)), dma((2, 2)),
             dma((2, wire_size - 1)), dma((2, wire_size - 1)),
             dma((2, wire_size - 1)), dma((2, wire_size - 1)),
             dma((2, chips - 1)), dma((2, chips - 1)),

time: 84.4 us -> 83.1 us (0.985)
  Pallas kernels: 72.1 us -> 70.7 us
    pallas_call x1, Pallas kernels: 72.1 us -> 70.7 us  [run(): pl.pallas_call(functools.partial(kernel, sizes, scale), out_shape=[jax.Sh...]
where the time goes in v6:
time: 83.1 us; the launch traced here: 82.9 us
  Pallas kernels  70.7 us (85%)
  local copies, waits for them, and re-layouts  5.17 us (6%)
  other arithmetic  4.19 us (5%)
  between operations  2.79 us (3%)
    pallas_call x1, Pallas kernels, run(): pl.pallas_call(functools.partial(kernel, sizes, scale), out_shape=[jax.Sh...  70.7 us
    slice x2, local copies, waits for them, and re-layouts, on_device(): return (placed[0], placed[1], weights[0], weights[1])  2.75 us

profile of v6, /device:TPU:1, one launch (start us, length us, event | category | flops | bytes accessed | tf_op | source)
XLA Modules:
  0.0 82.9 jit_solution(8866134755285056373)
XLA Ops:
  1.3 0.8 select_reduce_fusion.1
  2.1 1.3 %fusion = (s32[]{:T(128)}, s32[]{:T(128)}) fusion(pred[9]{0:T(512)(128)(4,1)} %constant.30.clone, pred[9]{0:T(512)(128)(4,1)} %constant.29.clone, s32[9]{0:T(128)S(1)} %select_reduce_fusion.1), kind=kLoop, calls=%fused_computation.19 | loop fusion | flops 61 | bytes 62 | tf_op jit(solution)/shard_map/reduce_sum | solution.py:452
  4.7 0.7 fusion.1
  5.4 0.1 select_reduce_fusion
  5.5 0.1 reshape.96
  5.6 0.1 broadcast_in_dim.72
  5.7 0.1 broadcast_in_dim.73
  5.8 1.0 %pad_maximum_fusion = bf16[2,9,64,128]{3,2,1,0:T(8,128)(2,1)S(1)} fusion(bf16[1,9,64,128]{3,2,1,0:T(8,128)(2,1)} %bitcast.49, bf16[1,9,64,128]{3,2,1,0:T(8,128)(2,1)} %bitcast.50), kind=kLoop, calls=%fused_computation.2 | loop fusion | flops 147456 | bytes 589824 | tf_op jit(solution)/shard_map/stack | solution.py:458
  6.8 0.6 gather_fusion
  7.4 0.1 bitcast_select_fusion.1
  7.5 0.1 copy.27
  7.8 0.1 copy.36
  7.9 0.1 pad.8.clone
  8.1 0.1 broadcast_in_dim.74
  8.2 70.7 %layers.1 = (bf16[2,768,128]{2,1,0:T(8,128)(2,1)S(1)}, bf16[2,3456,128]{2,1,0:T(8,128)(2,1)}) custom-call(bf16[2,768,128]{2,1,0:T(8,128)(2,1)S(1)} %bitcast.35, bf16[2,2,64,128]{3,2,1,0:T(8,128)(2,1)S(1)} %pad_maximum_fusion.1.x_ref, bf16[2,96,128]{2,1,0:T(8,128)(2,1)S(1)} %pad_maximum_fusion.2.y_ref, bf16[4,8,128]{2,1,0:T(8,128)(2,1)S(1)} %pad_maximum_fusion.3.c_ref, ...), custom_call_target="tpu_custom_call" | custom-call | tf_op jit(solution)/shard_map/layers/pallas_call | solution.py:402
  78.9 0.0 copy-start
  79.0 0.1 slice.72
  79.1 0.1 copy.35
  79.2 0.1 copy.34
  79.4 0.6 gather_fusion.1
  80.0 0.1 bitcast_select_fusion
  80.1 0.7 fusion.4
  80.8 0.0 copy-done
  80.8 2.0 %fusion.2 = (f32[1,3456,128]{2,1,0:T(8,128)}, f32[1,3456,128]{2,1,0:T(8,128)}) fusion(bf16[2,3456,128]{2,1,0:T(8,128)(2,1)S(1)} %copy-done), kind=kLoop, calls=%fused_computation.25 | loop fusion | bytes 7077888 | tf_op jit(solution)/shard_map/slice | solution.py:484
  (16 shorter events, 0.2 us)
Async XLA Ops:
  78.9 1.9 %copy-start = (bf16[2,3456,128]{2,1,0:T(8,128)(2,1)S(1)}, bf16[2,3456,128]{2,1,0:T(8,128)(2,1)}, u32[]{:S(2)}) copy-start(bf16[2,3456,128]{2,1,0:T(8,128)(2,1)} %get-tuple-element.8) | copy-start | bytes 5308420
